TPU v7x, 256 devices: a whole 4x4x8 slice. The times are simulated.
256 devices in a mesh: dp: 16 (over y, z_hi, core), pool: 16 (over x, z_lo).
Axes of the slice: x: 4, y: 4, z: 8 (z_hi: 2, z_lo: 4; z = z_hi * 4 + z_lo), core: 2. Of those that a mesh axis runs over, the one named last changes fastest.
Arguments:
- feats: bfloat16 [65536, 2048], P(('dp', 'pool')), may hold values from -24 to 24
- tower_w: bfloat16 [2048, 256], replicated, may hold values from -0.125 to 0.125
- partners: int32 [65536], P(('dp', 'pool')), may hold values from 0 to 4095, as said below
- popularity_buckets: int32 [65536], P(('dp', 'pool')), may hold values from 0 to 31
- row_counts: int32 [16, 16], replicated, may hold values from 64 to 256, as said below
Outputs:
- grad_w: float32 [2048, 256], P(('dp', 'pool'))
Inputs may be any that keep to these rules, and one draw needn't show every extreme that they name: row_counts[d, p] valid slots stand first in the block of 256 slots of pool member p in data group d; in every data group some member has all 256 slots valid. `partners`: each slot's partner is the position, within its data group's 4096 slots, of a valid slot other than itself.
All inputs are finite; a program needn't handle non-finite values.
Results may differ from a plain program's by a relative error of at most 0.0038.
The roundings to bfloat16 on the way count: a program that leaves them out, or rounds other values in their place, can miss the bound.
Values may be sent and summed in bfloat16 or wider, within the bound.
A program may use at most 64 MiB of HBM per device.

v0:
```python
import jax
import jax.numpy as jnp
from jax import lax
from jax.sharding import PartitionSpec as P

sharpness_scaler = 0.05
epsilon = 1e-06


def contract_rows(left, right):
    return lax.dot_general(
        left, right, (((0,), (0,)), ((), ())), preferred_element_type=jnp.float32
    )


def contract_cols(left, right):
    return lax.dot_general(
        left, right, (((1,), (1,)), ((), ())), preferred_element_type=jnp.float32
    )


def per_device(feats, tower_w, partners, popularity_buckets, row_counts):
    shard_rows = feats.shape[0]
    pool_size = lax.axis_size("pool")
    member = lax.axis_index("pool")
    group_index = lax.axis_index("dp")
    projected = jnp.dot(feats, tower_w, preferred_element_type=jnp.float32)
    inv_norm = lax.rsqrt(jnp.sum(projected * projected, axis=1, keepdims=True) + epsilon)
    normed = projected * inv_norm
    embedded = normed.astype(jnp.bfloat16)
    prior_occurrence_correction = (-(popularity_buckets.astype(jnp.float32) + 0.5) / 4.0).astype(
        jnp.bfloat16
    )
    all_emb, all_logq = (
        lax.all_gather(embedded, "pool", axis=0, tiled=True),
        lax.all_gather(prior_occurrence_correction, "pool", axis=0, tiled=True),
    )
    group_counts = lax.dynamic_index_in_dim(row_counts, group_index, 0, keepdims=False)
    own_count = lax.dynamic_index_in_dim(group_counts, member, 0, keepdims=False)
    local_rows = jnp.arange(shard_rows, dtype=jnp.int32)
    source_usable = local_rows < own_count
    row_index = member * shard_rows + local_rows
    col_valid = (local_rows[None, :] < group_counts[:, None]).reshape(-1)
    shards_per = min(pool_size, max(1, 512 // shard_rows))
    while pool_size % shards_per:
        shards_per = shards_per - 1
    block_width = shard_rows * shards_per
    block_count = pool_size // shards_per
    emb_blocks = all_emb.reshape(block_count, block_width, -1)
    logq_blocks = all_logq.astype(jnp.float32).reshape(block_count, block_width)
    valid_blocks = col_valid.reshape(block_count, block_width)
    first_cols = jnp.arange(block_count, dtype=jnp.int32) * block_width

    def segment_contributions(block_emb, tile_popularity_logarithm, block_valid, first_col):
        angular_affinities = contract_cols(embedded, block_emb)
        target_ordinal = first_col + jnp.arange(block_width, dtype=jnp.int32)
        admitted_flags = block_valid[None, :] & (row_index[:, None] != target_ordinal[None, :])
        natural_powers = jnp.where(
            admitted_flags,
            jnp.exp(angular_affinities / sharpness_scaler - tile_popularity_logarithm[None, :]),
            0.0,
        )
        return (angular_affinities, target_ordinal, natural_powers)

    def add_totals(running, operand_tensors):
        return (running + jnp.sum(segment_contributions(*operand_tensors)[2], axis=1), None)

    shared = (emb_blocks, logq_blocks, valid_blocks, first_cols)
    normalizer_sums, ignored = lax.scan(add_totals, jnp.zeros((shard_rows,), jnp.float32), shared)

    def source_multiplier(target_ordinal, natural_powers):
        matched_partner = (partners[:, None] == target_ordinal[None, :]).astype(jnp.float32)
        return jnp.where(
            source_usable[:, None], natural_powers / normalizer_sums[:, None] - matched_partner, 0.0
        ).astype(jnp.bfloat16)

    zero_grad = jnp.zeros(normed.shape, jnp.float32)

    def back_step(running, operand_tensors):
        angular_affinities, target_ordinal, natural_powers = segment_contributions(*operand_tensors)
        pair_multiplier = source_multiplier(target_ordinal, natural_powers)
        updated = running + jnp.dot(
            pair_multiplier, operand_tensors[0], preferred_element_type=jnp.float32
        )
        return (updated, contract_rows(pair_multiplier, embedded))

    row_term, col_terms = lax.scan(back_step, zero_grad, shared)
    own_term = lax.psum_scatter(
        col_terms.reshape(pool_size * shard_rows, -1), "pool", scatter_dimension=0, tiled=True
    )
    grad_emb = row_term + own_term
    grad_proj = (
        (grad_emb - normed * jnp.sum(normed * grad_emb, axis=1, keepdims=True)) * inv_norm
    ).astype(jnp.bfloat16)
    return lax.psum_scatter(
        contract_rows(feats, grad_proj), ("dp", "pool"), scatter_dimension=0, tiled=True
    )


def solution(mesh):
    return jax.shard_map(
        per_device,
        mesh=mesh,
        in_specs=(P(("dp", "pool"), None), P(), P(("dp", "pool")), P(("dp", "pool")), P()),
        out_specs=P(("dp", "pool"), None),
        check_vma=False,
    )
```

profile of v0, /device:TPU:6, one launch (start us, length us, event | category | flops | bytes accessed | tf_op | source)
XLA Modules:
  0.0 1546.3 jit_solution(15717707194933951272)
XLA Ops:
  6.5 1.2 copy-done
  7.8 1.8 multiply_reduce_fusion.1
  11.0 1.0 copy.26
  12.9 37.2 %all-gather = bf16[16,1,256]{2,1,0:T(2,128)(2,1)S(1)} all-gather(bf16[1,1,256]{2,1,0:T(2,128)(2,1)S(1)} %reshape.46), channel_id=1, replica_groups=mesh['dp'=16,'pool'=16] {'pool'}, dimensions={0}, use_global_device_ids=true | all-gather | bytes 8704 | tf_op jit(solution)/shard_map/all_gather | solution.py:36
  50.9 1.3 dynamic_slice.36
  52.7 43.0 %all-gather.3.cloned.1.call-done = bf16[4096,256]{0,1:T(8,128)(2,1)} async-done(((bf16[256,256]{0,1:T(8,128)(2,1)}), bf16[4096,256]{0,1:T(8,128)(2,1)}) %all-gather.3.cloned.1.call-update) | async-done | bytes 2097168 | tf_op jit(solution)/shard_map/all_gather | solution.py:35
  95.8 3.3 copy.33
  99.0 24.7 %while.24 = (s32[]{:T(128)}, f32[256]{0:T(256)S(1)}, pred[8,512]{1,0:T(8,128)(4,1)S(1)}, s32[8]{0:T(128)}, bf16[8,512,256]{2,1,0:T(8,128)(2,1)S(1)}, /*index=5*/...) while((s32[]{:T(128)}, f32[256]{0:T(256)S(1)}, ...), condition=%wide.region_3.4_spmd.clone, body=%wide.region_1.3_spmd.clone.sunk | while | flops 67896320 | bytes 411287 | solution.py:69
  99.1 1.3 dynamic_slice.75
  101.0 0.7 constant_dynamic-slice_fusion.4
  102.1 1.3 dynamic_slice.75
  104.1 0.7 constant_dynamic-slice_fusion.4
  105.2 1.3 dynamic_slice.75
  107.2 0.7 constant_dynamic-slice_fusion.4
  108.3 1.3 dynamic_slice.75
  111.4 1.3 dynamic_slice.75
  113.3 0.7 constant_dynamic-slice_fusion.4
  114.5 1.3 dynamic_slice.75
  116.4 0.7 constant_dynamic-slice_fusion.4
  117.6 1.3 dynamic_slice.75
  120.7 1.3 dynamic_slice.75
  122.6 0.7 constant_dynamic-slice_fusion.4
  123.8 40.8 %while.25 = (s32[]{:T(128)}, f32[256,256]{1,0:T(8,128)S(1)}, f32[8,512,256]{2,1,0:T(8,128)}, pred[8,512]{1,0:T(8,128)(4,1)S(1)}, s32[8]{0:T(128)}, /*index=5*/bf...) while((s32[]{:T(128)}, f32[256,256]{1,0:T(8,128)S(1)}, ...), condition=%wide.region_5.6_spmd.clone, body=%wide.region_4.5_spmd.clone.sunk | while | flops 202900480 | bytes 2638275 | solution.py:87
  123.8 1.3 dynamic_slice.80
  126.4 0.7 constant_dynamic-slice_fusion.5
  127.8 1.0 fusion.60
  128.9 1.3 dynamic_slice.80
  131.4 0.7 constant_dynamic-slice_fusion.5
  132.9 1.1 fusion.60
  134.0 1.3 dynamic_slice.80
  136.6 0.7 constant_dynamic-slice_fusion.5
  138.0 1.1 fusion.60
  139.1 1.3 dynamic_slice.80
  141.7 0.7 constant_dynamic-slice_fusion.5
  143.1 1.0 fusion.60
  144.2 1.3 dynamic_slice.80
  148.2 1.0 fusion.60
  149.3 1.3 dynamic_slice.80
  153.3 1.0 fusion.60
  154.4 1.3 dynamic_slice.80
  158.4 1.0 fusion.60
  159.5 1.3 dynamic_slice.80
  163.5 1.0 fusion.60
  164.6 5.6 copy.30
  170.4 101.6 %reduce-scatter.5.cloned.1.call-done = f32[256,256]{0,1:T(8,128)} async-done(((f32[4096,256]{0,1:T(8,128)}), f32[256,256]{0,1:T(8,128)}) %reduce-scatter.5.cloned.1.call-update) | async-done | bytes 262160 | tf_op jit(solution)/shard_map/reduce_scatter | solution.py:88
  272.0 1.0 multiply_reduce_fusion
  273.5 1.9 copy.31
  275.4 1264.3 %reduce-scatter.7.cloned.1.call-done = f32[8,256]{1,0:T(8,128)} async-done(((f32[2048,256]{1,0:T(8,128)}), f32[8,256]{1,0:T(8,128)}) %reduce-scatter.7.cloned.1.call-update) | async-done | bytes 8208 | tf_op jit(solution)/shard_map/reduce_scatter | solution.py:95
  (128 shorter events, 33.4 us)
Async XLA Ops:
  6.5 1.2 copy-start
  6.5 6.2 copy-start.3
  6.5 89.2 %all-gather.3.cloned.1.call-start = ((), (), s32[]{:S(2)}) async-start(), calls=%async_computation.2 | async-start | bytes 2228224 | tf_op jit(solution)/shard_map/all_gather | solution.py:35
  9.5 0.7 copy-start.1
  10.9 261.1 %reduce-scatter.5.cloned.1.call-start = ((), (), s32[]{:S(2)}) async-start(), calls=%async_computation.3 | async-start | bytes 4456448 | tf_op jit(solution)/shard_map/reduce_scatter | solution.py:88
  99.0 24.7 %copy-start.4 = (s32[256]{0:T(256)S(1)}, s32[256]{0:T(256)}, u32[]{:S(2)}) copy-start(s32[256]{0:T(256)} %param.11) | copy-start | bytes 3076
  170.2 101.8 %copy-start.2 = (f32[256,256]{0,1:T(8,128)S(1)}, f32[256,256]{0,1:T(8,128)}, u32[]{:S(2)}) copy-start(f32[256,256]{0,1:T(8,128)} %copy-done.1) | copy-start | bytes 786436
  170.3 1369.5 %reduce-scatter.7.cloned.1.call-start = ((), (), s32[]{:S(2)}) async-start(), calls=%async_computation.4 | async-start | bytes 2105344 | tf_op jit(solution)/shard_map/reduce_scatter | solution.py:95
Sparse Core Ops, SparseCore 0:
  11.0 84.6 all-gather.2
  170.4 101.5 reduce-scatter.4
  275.5 1264.1 reduce-scatter.6
where the time goes:
time: 1570 us; the launch traced here: 1550 us
  waiting for transfers between devices  1410 us (90%)
  local copies, waits for them, and re-layouts  48.9 us (3%)
  blocking collectives  37.2 us (2%)
  matrix products  19.5 us (1%)
  other arithmetic  17.7 us (1%)
    reduce_scatter x1, waiting for transfers between devices, per_device(): lax.psum_scatter(contract_rows(feats, grad_proj), ('dp', 'pool'), scatter...  1260 us
    reduce_scatter x1, waiting for transfers between devices, per_device(): lax.psum_scatter(col_terms.reshape(pool_size * shard_rows, -1), 'pool', s...  102 us
    all_gather x1, waiting for transfers between devices, per_device(): lax.all_gather(embedded, 'pool', axis=0, tiled=True)  43 us
    all_gather x1, blocking collectives, per_device(): lax.all_gather(prior_occurrence_correction, 'pool', axis=0, tiled=True)  37.2 us
    dynamic_slice x48, local copies, waits for them, and re-layouts, per_device(): lax.scan(add_totals, jnp.zeros((shard_rows,), jnp.float32), shared)  32.2 us
  transfers between devices with their start and end apart: 3, of which 3 were waited for; matrix products, arithmetic and copies ran while one was open for 0% of the time, Pallas kernels for 0%

commit v1 on v0

v1 whole, which is shorter than its diff:
```python
import functools

import jax
import jax.numpy as jnp
from jax import lax
from jax.experimental import pallas as pl
from jax.experimental.pallas import tpu as pltpu
from jax.sharding import PartitionSpec as P

MESH = pl.DeviceIdType.MESH
EPS = 1e-06
SCALE = 28.853900817779268
ROWS = 256
HALF = 128
DE = 256
DIN = 2048
KC = 4
KW = DIN // KC


def nt(left, right):
    return lax.dot_general(
        left, right, (((1,), (1,)), ((), ())), preferred_element_type=jnp.float32
    )


def nn(left, right):
    return jnp.dot(left, right, preferred_element_type=jnp.float32)


def kernel(
    feats_hbm, w_hbm, part_ref, buck_ref, counts_ref, out_ref,
    feats_v, w_v, feats_t, e_all, p_all, meta, recips,
    normed_s, inv_s, own_w, own_part, own_valid, tot_s, g_s,
    core_send, core_recv, send2, recv2, acc2, send3, recv3, send4, recv4,
    in_sem, meta_ssem, meta_rsem, e_ssem, e_rsem, r_ssem, r_rsem,
    c_ssem, c_rsem, s2_sem, r2_sem, s3_sem, r3_sem, s4_sem, r4_sem,
):
    dp = lax.axis_index("dp")
    pool = lax.axis_index("pool")
    y = dp // 4
    zh = (dp // 2) % 2
    core = dp % 2
    x = pool // 4
    z = pool % 4

    loads = []
    for k in range(KC):
        cols = pl.ds(k * KW, KW)
        a = pltpu.make_async_copy(feats_hbm.at[:, cols], feats_v.at[:, cols], in_sem.at[k, 0])
        b = pltpu.make_async_copy(w_hbm.at[cols, :], w_v.at[cols, :], in_sem.at[k, 1])
        a.start()
        b.start()
        loads.append((a, b))

    barrier = pltpu.get_barrier_semaphore()

    def greet(d, p):
        pl.semaphore_signal(barrier, inc=1, device_id=(d, p), device_id_type=MESH)

    for k in range(1, 16):
        greet(dp, (pool + k) % 16)
    greet(y * 4 + zh * 2 + (1 - core), pool)
    for k in range(1, 4):
        greet(((y + k) % 4) * 4 + zh * 2 + core, pool)
    for k in range(4):
        greet(y * 4 + (1 - zh) * 2 + core, x * 4 + k)

    cnt = counts_ref[dp, pool]
    lane = lax.broadcasted_iota(jnp.int32, (1, ROWS), 1)
    valid = lane < cnt
    part_l = jnp.where(valid, part_ref[...], -1).astype(jnp.float32)
    w_l = jnp.where(valid, jnp.exp((buck_ref[...].astype(jnp.float32) + 0.5) * 0.25), 0.0)
    meta[pool, 0:1, :] = part_l
    meta[pool, 1:2, :] = w_l
    own_part[...] = jnp.broadcast_to(part_l, (128, ROWS)).T
    own_w[...] = jnp.broadcast_to(w_l, (128, ROWS)).T
    own_valid[...] = jnp.broadcast_to(jnp.where(valid, 1.0, 0.0), (128, ROWS)).T

    projected = None
    for k in range(KC):
        loads[k][0].wait()
        loads[k][1].wait()
        cols = pl.ds(k * KW, KW)
        term = nn(feats_v[:, cols], w_v[cols, :])
        projected = term if projected is None else projected + term
    inv_norm = lax.rsqrt(jnp.sum(projected * projected, axis=1, keepdims=True) + EPS)
    normed = projected * inv_norm
    normed_s[...] = normed
    inv_s[...] = jnp.broadcast_to(inv_norm, (ROWS, 128))
    e_all[pool] = normed.astype(jnp.bfloat16)

    pl.semaphore_wait(barrier, 23)

    pending = []
    for k in range(1, 16):
        c = pltpu.make_async_remote_copy(
            src_ref=meta.at[pool], dst_ref=meta.at[pool],
            send_sem=meta_ssem.at[k], recv_sem=meta_rsem.at[pool],
            device_id=(dp, (pool + k) % 16), device_id_type=MESH,
        )
        c.start()
        pending.append(c)

    def rows_of(h):
        return pl.ds(h * HALF, HALF)

    def send(slot, h, target, n):
        c = pltpu.make_async_remote_copy(
            src_ref=e_all.at[slot, rows_of(h)], dst_ref=e_all.at[slot, rows_of(h)],
            send_sem=e_ssem.at[n], recv_sem=e_rsem.at[slot, h],
            device_id=(dp, target), device_id_type=MESH,
        )
        c.start()
        pending.append(c)

    def arrive(slot, h):
        pltpu.make_async_remote_copy(
            src_ref=e_all.at[slot, rows_of(h)], dst_ref=e_all.at[slot, rows_of(h)],
            send_sem=e_ssem.at[0], recv_sem=e_rsem.at[slot, h],
            device_id=(dp, pool), device_id_type=MESH,
        ).wait_recv()

    def meta_arrive(slot):
        pltpu.make_async_remote_copy(
            src_ref=meta.at[slot], dst_ref=meta.at[slot],
            send_sem=meta_ssem.at[0], recv_sem=meta_rsem.at[slot],
            device_id=(dp, pool), device_id_type=MESH,
        ).wait_recv()

    zs = [z, z + 1 - 2 * (z % 2), (z + 2) % 4, 3 - z]
    right = (x + 1) % 4
    left = (x + 3) % 4
    far = (x + 2) % 4
    count = iter(range(64))

    def spread(slot, halves):
        for h in halves:
            send(slot, h, right * 4 + z, next(count))
            send(slot, 1 - h, left * 4 + z, next(count))

    spread(pool, (0, 1))
    for c in (1, 2, 3):
        for h in (0, 1):
            send(pool, h, x * 4 + zs[c], next(count))

    def scores(slot, first=False):
        s = nt(e_all[pool], e_all[slot])
        e = jnp.exp2(s * SCALE)
        if first:
            ri = lax.broadcasted_iota(jnp.int32, (ROWS, ROWS), 0)
            ci = lax.broadcasted_iota(jnp.int32, (ROWS, ROWS), 1)
            e = jnp.where(ri == ci, 0.0, e)
        p_all[slot] = e
        t = e * meta[slot, 1:2, :]
        t = t[:, :128] + t[:, 128:]
        if first:
            tot_s[...] = t
        else:
            tot_s[...] += t

    scores(pool, True)

    def transposes(lo, hi):
        for m in range(lo, hi):
            my, mz, mc = m // 4, (m // 2) % 2, m % 2
            t = feats_v[:, m * 128:(m + 1) * 128].T
            which = (mc + core) % 2
            for mx in range(4):
                at = (my * (8 - 6 * mc) + mx * (2 + 6 * mc) + mz) * 32
                feats_t[which, at:at + 32, :] = t[mx * 32:(mx + 1) * 32]

    transposes(0, 8)

    for c in range(4):
        if c < 3:
            nslot = x * 4 + zs[c + 1]
            for h in (0, 1):
                arrive(nslot, h)
                send(nslot, h, right * 4 + z, next(count))
                send(nslot, h, left * 4 + z, next(count))
        ls = left * 4 + zs[c]
        rs = right * 4 + zs[c]
        arrive(ls, 0)
        send(ls, 0, right * 4 + z, next(count))
        arrive(rs, 1)
        send(rs, 1, left * 4 + z, next(count))
        if c == 0:
            transposes(8, 16)
        if c < 3:
            meta_arrive(nslot)
            scores(nslot)
        arrive(ls, 1)
        meta_arrive(ls)
        scores(ls)
        arrive(rs, 0)
        meta_arrive(rs)
        scores(rs)
        if c > 0:
            fs = far * 4 + zs[c - 1]
            arrive(fs, 0)
            arrive(fs, 1)
            meta_arrive(fs)
            scores(fs)
    fs = far * 4 + zs[3]
    arrive(fs, 0)
    arrive(fs, 1)
    meta_arrive(fs)
    scores(fs)

    total = jnp.broadcast_to(jnp.sum(tot_s[...], axis=1, keepdims=True), (ROWS, 128))
    recip_own = own_valid[...] / total
    recips[pool] = recip_own.T[0:1, :]
    for k in range(1, 16):
        c = pltpu.make_async_remote_copy(
            src_ref=recips.at[pool], dst_ref=recips.at[pool],
            send_sem=r_ssem.at[k], recv_sem=r_rsem.at[pool],
            device_id=(dp, (pool + k) % 16), device_id_type=MESH,
        )
        c.start()
        pending.append(c)

    wide = lambda v: jnp.concatenate([v, v], axis=1)
    tot_s[...] = recip_own
    g_s[...] = jnp.zeros_like(g_s)
    lane_f = lax.broadcasted_iota(jnp.int32, (ROWS, ROWS), 1).astype(jnp.float32)
    row_f = lax.broadcasted_iota(jnp.int32, (ROWS, ROWS), 0).astype(jnp.float32)

    def row_term(s, carry):
        base = (s * ROWS).astype(jnp.float32)
        hit = wide(own_part[...]) == lane_f + base
        coef = p_all[s] * meta[s, 1:2, :] * wide(tot_s[...]) - jnp.where(hit, 1.0, 0.0)
        g_s[...] += nn(coef.astype(jnp.bfloat16), e_all[s])
        return carry

    lax.fori_loop(0, 16, row_term, 0)

    for k in range(1, 16):
        slot = (pool + k) % 16
        pltpu.make_async_remote_copy(
            src_ref=recips.at[slot], dst_ref=recips.at[slot],
            send_sem=r_ssem.at[0], recv_sem=r_rsem.at[slot],
            device_id=(dp, pool), device_id_type=MESH,
        ).wait_recv()

    mine = (pool * ROWS).astype(jnp.float32)

    def col_term(s, carry):
        hit = meta[s, 0:1, :] == row_f + mine
        coef = p_all[s] * wide(own_w[...]) * recips[s] - jnp.where(hit, 1.0, 0.0)
        g_s[...] += nn(coef.astype(jnp.bfloat16), e_all[s])
        return carry

    lax.fori_loop(0, 16, col_term, 0)

    g = g_s[...]
    nrm = normed_s[...]
    g = (g - nrm * jnp.sum(nrm * g, axis=1, keepdims=True)) * wide(inv_s[...])
    gp = g.astype(jnp.bfloat16)

    a_own = y * (1 - core) + x * core
    b_own = x * (1 - core) + y * core
    for t in (2, 1, 3, 0):
        a = (b_own + t) % 4
        core_send[a] = nn(feats_t[1, pl.ds(pl.multiple_of(a * 256, 256), 256), :], gp).astype(core_send.dtype)
        c = pltpu.make_async_remote_copy(
            src_ref=core_send.at[a], dst_ref=core_recv.at[a],
            send_sem=c_ssem.at[a], recv_sem=c_rsem.at[a],
            device_id=(y * 4 + zh * 2 + (1 - core), pool), device_id_type=MESH,
        )
        c.start()
        pending.append(c)
    for t in (2, 1, 3, 0):
        a = (a_own + t) % 4
        own = nn(feats_t[0, pl.ds(pl.multiple_of(a * 256, 256), 256), :], gp)
        pltpu.make_async_remote_copy(
            src_ref=core_send.at[a], dst_ref=core_recv.at[a],
            send_sem=c_ssem.at[a], recv_sem=c_rsem.at[a],
            device_id=(dp, pool), device_id_type=MESH,
        ).wait_recv()
        own = own + core_recv[a].astype(jnp.float32)
        if t:
            send2[a] = own.astype(send2.dtype)
            ty = a * (1 - core) + y * core
            tx = x * (1 - core) + a * core
            c = pltpu.make_async_remote_copy(
                src_ref=send2.at[a], dst_ref=recv2.at[a_own],
                send_sem=s2_sem.at[a], recv_sem=r2_sem.at[a_own],
                device_id=(ty * 4 + zh * 2 + core, tx * 4 + z), device_id_type=MESH,
            )
            c.start()
            pending.append(c)
        else:
            for q in range(4):
                acc2[q] = own[q * 64:(q + 1) * 64]
    for t in (1, 3, 2):
        a = (a_own + t) % 4
        pltpu.make_async_remote_copy(
            src_ref=send2.at[a], dst_ref=recv2.at[a],
            send_sem=s2_sem.at[a], recv_sem=r2_sem.at[a],
            device_id=(dp, pool), device_id_type=MESH,
        ).wait_recv()
    for t in (2, 1, 3, 0):
        b = (b_own + t) % 4
        part = acc2[b]
        rows = pl.ds(pl.multiple_of(b * 64, 64), 64)
        for u in (1, 2, 3):
            part = part + recv2[(a_own + u) % 4, rows, :].astype(jnp.float32)
        send3[b] = part.astype(send3.dtype)
        if t:
            ty = y * (1 - core) + b * core
            tx = b * (1 - core) + x * core
            c = pltpu.make_async_remote_copy(
                src_ref=send3.at[b], dst_ref=recv3.at[b_own],
                send_sem=s3_sem.at[b], recv_sem=r3_sem.at[b_own],
                device_id=(ty * 4 + zh * 2 + core, tx * 4 + z), device_id_type=MESH,
            )
            c.start()
            pending.append(c)
    part = send3[b_own]
    for t in (1, 3, 2):
        b = (b_own + t) % 4
        pltpu.make_async_remote_copy(
            src_ref=send3.at[b], dst_ref=recv3.at[b],
            send_sem=s3_sem.at[b], recv_sem=r3_sem.at[b],
            device_id=(dp, pool), device_id_type=MESH,
        ).wait_recv()
        part = part + recv3[b]
    for q in range(8):
        send4[q] = part[q * 8:(q + 1) * 8]
    zz = zh * 4 + z
    for t in (4, 3, 5, 2, 6, 1, 7):
        q = (zz + t) % 8
        c = pltpu.make_async_remote_copy(
            src_ref=send4.at[q], dst_ref=recv4.at[zz],
            send_sem=s4_sem.at[q], recv_sem=r4_sem.at[zz],
            device_id=(y * 4 + (q // 4) * 2 + core, x * 4 + q % 4), device_id_type=MESH,
        )
        c.start()
        pending.append(c)
    result = send4[zz]
    for t in (1, 7, 2, 6, 3, 5, 4):
        q = (zz + t) % 8
        pltpu.make_async_remote_copy(
            src_ref=send4.at[q], dst_ref=recv4.at[q],
            send_sem=s4_sem.at[q], recv_sem=r4_sem.at[q],
            device_id=(dp, pool), device_id_type=MESH,
        ).wait_recv()
        result = result + recv4[q]
    out_ref[...] = result
    for c in pending:
        c.wait_send()


def per_device(feats, tower_w, partners, popularity_buckets, row_counts):
    f32, bf16 = jnp.float32, jnp.bfloat16
    vmem = pltpu.VMEM
    dma = pltpu.SemaphoreType.DMA
    return pl.pallas_call(
        kernel,
        out_shape=jax.ShapeDtypeStruct((8, DE), f32),
        in_specs=[
            pl.BlockSpec(memory_space=pl.ANY),
            pl.BlockSpec(memory_space=pl.ANY),
            pl.BlockSpec(memory_space=pltpu.VMEM),
            pl.BlockSpec(memory_space=pltpu.VMEM),
            pl.BlockSpec(memory_space=pltpu.SMEM),
        ],
        out_specs=pl.BlockSpec(memory_space=pltpu.VMEM),
        scratch_shapes=[
            vmem((ROWS, DIN), bf16),
            vmem((DIN, DE), bf16),
            vmem((2, 1024, ROWS), bf16),
            vmem((16, ROWS, DE), bf16),
            vmem((16, ROWS, ROWS), f32),
            vmem((16, 2, ROWS), f32),
            vmem((16, 1, ROWS), f32),
            vmem((ROWS, DE), f32),
            vmem((ROWS, 128), f32),
            vmem((ROWS, 128), f32),
            vmem((ROWS, 128), f32),
            vmem((ROWS, 128), f32),
            vmem((ROWS, 128), f32),
            vmem((ROWS, DE), f32),
            vmem((4, 256, DE), bf16),
            vmem((4, 256, DE), bf16),
            vmem((4, 256, DE), bf16),
            vmem((4, 256, DE), bf16),
            vmem((4, 64, DE), f32),
            vmem((4, 64, DE), f32),
            vmem((4, 64, DE), f32),
            vmem((8, 8, DE), f32),
            vmem((8, 8, DE), f32),
            dma((KC, 2)),
            dma((16,)),
            dma((16,)),
            dma((32,)),
            dma((16, 2)),
            dma((16,)),
            dma((16,)),
            dma((4,)),
            dma((4,)),
            dma((4,)),
            dma((4,)),
            dma((4,)),
            dma((4,)),
            dma((8,)),
            dma((8,)),
        ],
        compiler_params=pltpu.CompilerParams(collective_id=0, has_side_effects=True),
    )(feats, tower_w, partners.reshape(1, ROWS), popularity_buckets.reshape(1, ROWS), row_counts)


def solution(mesh):
    return jax.shard_map(
        per_device,
        mesh=mesh,
        in_specs=(P(("dp", "pool"), None), P(), P(("dp", "pool")), P(("dp", "pool")), P()),
        out_specs=P(("dp", "pool"), None),
        check_vma=False,
    )
```

time: 1570 us -> 62.1 us (0.04); the launches traced: 1550 us -> 61.4 us
  waiting for transfers between devices: 1410 us -> 0 us
  Pallas kernels: 0 us -> 60.1 us
  local copies, waits for them, and re-layouts: 48.9 us -> 1.3 us
  blocking collectives: 37.2 us -> 0 us
  matrix products: 19.5 us -> 0 us
  other arithmetic: 17.7 us -> 0 us
    reduce_scatter x2 -> x0, waiting for transfers between devices: 1370 us -> none  [the longest x1 1260 us: per_device(): lax.psum_scatter(contract_rows(feats, grad_proj), ('dp', 'pool'), scatter...]
    pallas_call x0 -> x1, Pallas kernels: none -> 60.1 us  [per_device(): pl.pallas_call(kernel, out_shape=jax.ShapeDtypeStruct((8, DE), f32), in_s...]
    all_gather x1 -> x0, waiting for transfers between devices: 43 us -> none  [per_device(): lax.all_gather(embedded, 'pool', axis=0, tiled=True)]
    all_gather x1 -> x0, blocking collectives: 37.2 us -> none  [per_device(): lax.all_gather(prior_occurrence_correction, 'pool', axis=0, tiled=True)]
    dynamic_slice x50 -> x0, local copies, waits for them, and re-layouts: 34.2 us -> none  [the longest x48 32.2 us: per_device(): lax.scan(add_totals, jnp.zeros((shard_rows,), jnp.float32), shared)]
    dot_general x34 -> x0, matrix products: 19.5 us -> none  [the longest x9 8.76 us: contract_rows(): lax.dot_general(left, right, (((0,), (0,)), ((), ())), preferred_element_...]
  transfers between devices with their start and end apart: 3 -> 0, of which waited for: 3 -> 0; matrix products, arithmetic and copies ran while one was open for 0% -> 0% of each run, Pallas kernels for 0% -> 0%
where the time goes in v1:
time: 62.1 us; the launch traced here: 61.4 us
  Pallas kernels  60.1 us (97%)
  local copies, waits for them, and re-layouts  1.3 us (2%)
    pallas_call x1, Pallas kernels, per_device(): pl.pallas_call(kernel, out_shape=jax.ShapeDtypeStruct((8, DE), f32), in_s...  60.1 us
    unnamed x1, local copies, waits for them, and re-layouts  1.3 us

profile of v1, /device:TPU:6, one launch (start us, length us, event | category | flops | bytes accessed | tf_op | source)
XLA Modules:
  0.0 61.4 jit_solution(5823387437739126040)
XLA Ops:
  0.0 60.1 %shard_map.55 = f32[8,256]{1,0:T(8,128)} custom-call(bf16[256,2048]{1,0:T(8,128)(2,1)} %feats_hbm.1, bf16[2048,256]{1,0:T(8,128)(2,1)} %w_hbm.1, s32[1,256]{1,0:T(1,128)} %bitcast.2, s32[1,256]{1,0:T(1,128)} %bitcast.3, s32[16,16]{1,0:T(8,128)} %counts_ref.1), custom_call_target="tpu_custom_call" | custom-call | tf_op jit(solution)/shard_map/pallas_call | solution.py:359
  60.1 1.3 %copy.7 = f32[8,256]{1,0:T(8,128)} copy(f32[8,256]{1,0:T(8,128)} %shard_map.55) | data formatting | bytes 16384

commit v2 on v1

v2 whole, which is shorter than its diff:
```python
import functools

import jax
import jax.numpy as jnp
from jax import lax
from jax.experimental import pallas as pl
from jax.experimental.pallas import tpu as pltpu
from jax.sharding import PartitionSpec as P

MESH = pl.DeviceIdType.MESH
EPS = 1e-06
SCALE = 28.853900817779268
ROWS = 256
HALF = 128
DE = 256
DIN = 2048
KC = 4
KW = DIN // KC


def nt(left, right):
    return lax.dot_general(
        left, right, (((1,), (1,)), ((), ())), preferred_element_type=jnp.float32
    )


def nn(left, right):
    return jnp.dot(left, right, preferred_element_type=jnp.float32)


def kernel(
    feats_hbm, w_hbm, part_hbm, buck_hbm, counts_hbm, out_ref,
    feats_v, w_v, part_v, buck_v, counts_v, feats_t, e_all, a_all, b_all, meta, recips,
    normed_s, inv_s, own_w, own_part, own_valid, tot_s, g_s,
    core_send, core_recv, keep2, send2, recv2, send3, recv3, send4, recv4,
    in_sem, small_sem, meta_ssem, meta_rsem, e_ssem, e_rsem, r_ssem, r_rsem,
    c_ssem, c_rsem, s2_sem, r2_sem, s3_sem, r3_sem, s4_sem, r4_sem,
):
    dp = lax.axis_index("dp")
    pool = lax.axis_index("pool")
    y = dp // 4
    zh = (dp // 2) % 2
    core = dp % 2
    x = pool // 4
    z = pool % 4
    zs = [z, z + 1 - 2 * (z % 2), (z + 2) % 4, 3 - z]

    barrier = pltpu.get_barrier_semaphore()

    def greet(d, p):
        pl.semaphore_signal(barrier, inc=1, device_id=(d, p), device_id_type=MESH)

    for k in range(1, 16):
        greet(dp, (pool + k) % 16)
    greet(y * 4 + zh * 2 + (1 - core), pool)
    for k in range(1, 4):
        greet(((y + k) % 4) * 4 + zh * 2 + core, pool)
    for k in range(4):
        greet(y * 4 + (1 - zh) * 2 + core, x * 4 + k)

    loads = []
    for k in range(KC):
        cols = pl.ds(k * KW, KW)
        a = pltpu.make_async_copy(feats_hbm.at[:, cols], feats_v.at[:, cols], in_sem.at[k, 0])
        b = pltpu.make_async_copy(w_hbm.at[cols, :], w_v.at[cols, :], in_sem.at[k, 1])
        a.start()
        b.start()
        loads.append((a, b))
    small = [
        pltpu.make_async_copy(part_hbm, part_v, small_sem.at[0]),
        pltpu.make_async_copy(buck_hbm, buck_v, small_sem.at[1]),
        pltpu.make_async_copy(counts_hbm, counts_v, small_sem.at[2]),
    ]
    for c in small:
        c.start()

    projected = None
    for k in range(KC):
        loads[k][0].wait()
        loads[k][1].wait()
        cols = pl.ds(k * KW, KW)
        term = nn(feats_v[:, cols], w_v[cols, :])
        projected = term if projected is None else projected + term
    inv_norm = lax.rsqrt(jnp.sum(projected * projected, axis=1, keepdims=True) + EPS)
    normed = projected * inv_norm
    normed_s[...] = normed
    inv_s[...] = jnp.broadcast_to(inv_norm, (ROWS, 128))
    e_all[pool] = normed.astype(jnp.bfloat16)

    for c in small:
        c.wait()
    cnt = counts_v[dp, pool]
    lane = lax.broadcasted_iota(jnp.int32, (1, ROWS), 1)
    valid = lane < cnt
    part_l = jnp.where(valid, part_v[...], -1).astype(jnp.float32)
    w_l = jnp.where(valid, jnp.exp((buck_v[...].astype(jnp.float32) + 0.5) * 0.25), 0.0)
    meta[pool, 0:1, :] = part_l
    meta[pool, 1:2, :] = w_l

    pl.semaphore_wait(barrier, 23)

    pending = []

    def rows_of(h):
        return pl.ds(h * HALF, HALF)

    def send(slot, h, target, n):
        c = pltpu.make_async_remote_copy(
            src_ref=e_all.at[slot, rows_of(h)], dst_ref=e_all.at[slot, rows_of(h)],
            send_sem=e_ssem.at[n], recv_sem=e_rsem.at[slot, h],
            device_id=(dp, target), device_id_type=MESH,
        )
        c.start()
        pending.append(c)

    def arrive(slot, h):
        pltpu.make_async_remote_copy(
            src_ref=e_all.at[slot, rows_of(h)], dst_ref=e_all.at[slot, rows_of(h)],
            send_sem=e_ssem.at[0], recv_sem=e_rsem.at[slot, h],
            device_id=(dp, pool), device_id_type=MESH,
        ).wait_recv()

    def meta_arrive(slot):
        pltpu.make_async_remote_copy(
            src_ref=meta.at[slot], dst_ref=meta.at[slot],
            send_sem=meta_ssem.at[0], recv_sem=meta_rsem.at[slot],
            device_id=(dp, pool), device_id_type=MESH,
        ).wait_recv()

    right = (x + 1) % 4
    left = (x + 3) % 4
    far = (x + 2) % 4
    count = iter(range(64))
    for h in (0, 1):
        send(pool, h, right * 4 + z, next(count))
        send(pool, 1 - h, left * 4 + z, next(count))
    for c in (1, 2, 3):
        for h in (0, 1):
            send(pool, h, x * 4 + zs[c], next(count))
    for k in range(1, 16):
        c = pltpu.make_async_remote_copy(
            src_ref=meta.at[pool], dst_ref=meta.at[pool],
            send_sem=meta_ssem.at[k], recv_sem=meta_rsem.at[pool],
            device_id=(dp, (pool + k) % 16), device_id_type=MESH,
        )
        c.start()
        pending.append(c)

    own_part[...] = jnp.broadcast_to(part_l, (128, ROWS)).T
    own_w[...] = jnp.broadcast_to(w_l, (128, ROWS)).T
    own_valid[...] = jnp.broadcast_to(jnp.where(valid, 1.0, 0.0), (128, ROWS)).T

    def wide(v):
        return jnp.concatenate([v, v], axis=1)

    def scores(slot, first=False):
        s = nt(e_all[pool], e_all[slot])
        e = jnp.exp2(s * SCALE)
        if first:
            ri = lax.broadcasted_iota(jnp.int32, (ROWS, ROWS), 0)
            ci = lax.broadcasted_iota(jnp.int32, (ROWS, ROWS), 1)
            e = jnp.where(ri == ci, 0.0, e)
        b_all[slot] = e * wide(own_w[...])
        t = e * meta[slot, 1:2, :]
        a_all[slot] = t
        t = t[:, :128] + t[:, 128:]
        if first:
            tot_s[...] = t
        else:
            tot_s[...] += t

    scores(pool, True)

    def transposes(lo, hi):
        for m in range(lo, hi):
            my, mz, mc = m // 4, (m // 2) % 2, m % 2
            t = feats_v[:, m * 128:(m + 1) * 128].T
            which = (mc + core) % 2
            for mx in range(4):
                at = (my * (2 + 6 * mc) + mx * (8 - 6 * mc) + mz) * 32
                feats_t[which, at:at + 32, :] = t[mx * 32:(mx + 1) * 32]

    transposes(0, 8)

    for c in range(4):
        if c < 3:
            nslot = x * 4 + zs[c + 1]
            for h in (0, 1):
                arrive(nslot, h)
                send(nslot, h, right * 4 + z, next(count))
                send(nslot, h, left * 4 + z, next(count))
        ls = left * 4 + zs[c]
        rs = right * 4 + zs[c]
        arrive(ls, 0)
        send(ls, 0, right * 4 + z, next(count))
        arrive(rs, 1)
        send(rs, 1, left * 4 + z, next(count))
        if c == 0:
            transposes(8, 16)
        if c < 3:
            meta_arrive(nslot)
            scores(nslot)
        arrive(ls, 1)
        meta_arrive(ls)
        scores(ls)
        arrive(rs, 0)
        meta_arrive(rs)
        scores(rs)
        if c > 0:
            fs = far * 4 + zs[c - 1]
            arrive(fs, 0)
            arrive(fs, 1)
            meta_arrive(fs)
            scores(fs)
    fs = far * 4 + zs[3]
    arrive(fs, 0)
    arrive(fs, 1)
    meta_arrive(fs)
    scores(fs)

    order = [
        [(2, 3), (2, 2), (2, 1), (3, 3)],
        [(1, 3), (3, 2), (1, 2), (2, 0)],
        [(3, 1), (1, 1), (0, 3), (0, 2)],
        [(3, 0), (1, 0), (0, 1), (0, 0)],
    ]

    def member(dx, c):
        return ((x + dx) % 4) * 4 + zs[c]

    total = jnp.broadcast_to(jnp.sum(tot_s[...], axis=1, keepdims=True), (ROWS, 128))
    recip_own = own_valid[...] / total
    recips[pool] = recip_own.T[0:1, :]
    n = 0
    for group in order:
        for dx, c in group:
            if (dx, c) == (0, 0):
                continue
            cp = pltpu.make_async_remote_copy(
                src_ref=recips.at[pool], dst_ref=recips.at[pool],
                send_sem=r_ssem.at[n], recv_sem=r_rsem.at[pool],
                device_id=(dp, member(dx, c)), device_id_type=MESH,
            )
            cp.start()
            pending.append(cp)
            n += 1

    tot_s[...] = recip_own
    g_s[...] = jnp.zeros_like(g_s)
    lane_f = lax.broadcasted_iota(jnp.int32, (1, ROWS), 1).astype(jnp.float32)

    def row_term(i, carry):
        acc = None
        for j in range(4):
            s = i * 4 + j
            hit = wide(own_part[...]) == lane_f + (s * ROWS).astype(jnp.float32)
            coef = a_all[s] * wide(tot_s[...])
            coef = jnp.where(hit, coef - 1.0, coef).astype(jnp.bfloat16)
            term = nn(coef, e_all[s])
            acc = term if acc is None else acc + term
        g_s[...] += acc
        return carry

    lax.fori_loop(0, 4, row_term, 0)

    mine = lax.broadcasted_iota(jnp.int32, (ROWS, 128), 0).astype(jnp.float32) + (pool * ROWS).astype(jnp.float32)
    own_part[...] = mine
    for group in order[::-1]:
        slots = [member(dx, c) for dx, c in group[::-1]]
        for (dx, c), s in zip(group[::-1], slots):
            if (dx, c) == (0, 0):
                continue
            pltpu.make_async_remote_copy(
                src_ref=recips.at[s], dst_ref=recips.at[s],
                send_sem=r_ssem.at[0], recv_sem=r_rsem.at[s],
                device_id=(dp, pool), device_id_type=MESH,
            ).wait_recv()
        acc = None
        for s in slots:
            hit = wide(own_part[...]) == meta[s, 0:1, :]
            coef = b_all[s] * recips[s]
            coef = jnp.where(hit, coef - 1.0, coef).astype(jnp.bfloat16)
            term = nn(coef, e_all[s])
            acc = term if acc is None else acc + term
        g_s[...] += acc

    g = g_s[...]
    nrm = normed_s[...]
    g = (g - nrm * jnp.sum(nrm * g, axis=1, keepdims=True)) * wide(inv_s[...])
    gp = g.astype(jnp.bfloat16)

    a_own = y * (1 - core) + x * core
    b_own = x * (1 - core) + y * core
    turns = (2, 1, 3, 0)
    for t in turns:
        b = (a_own + t) % 4
        core_send[b] = nn(feats_t[1, pl.ds(pl.multiple_of(b * 256, 256), 256), :], gp).astype(core_send.dtype)
        c = pltpu.make_async_remote_copy(
            src_ref=core_send.at[b], dst_ref=core_recv.at[b],
            send_sem=c_ssem.at[b], recv_sem=c_rsem.at[b],
            device_id=(y * 4 + zh * 2 + (1 - core), pool), device_id_type=MESH,
        )
        c.start()
        pending.append(c)
    for t in turns:
        b = (b_own + t) % 4
        own = nn(feats_t[0, pl.ds(pl.multiple_of(b * 256, 256), 256), :], gp)
        pltpu.make_async_remote_copy(
            src_ref=core_send.at[b], dst_ref=core_recv.at[b],
            send_sem=c_ssem.at[b], recv_sem=c_rsem.at[b],
            device_id=(dp, pool), device_id_type=MESH,
        ).wait_recv()
        own = own + core_recv[b].astype(jnp.float32)
        for q in range(4):
            keep2[b, q] = own[q * 64:(q + 1) * 64]
            send2[b, q] = own[q * 64:(q + 1) * 64].astype(send2.dtype)
        for u in (2, 1, 3):
            a = (a_own + u) % 4
            ty = a * (1 - core) + y * core
            tx = x * (1 - core) + a * core
            c = pltpu.make_async_remote_copy(
                src_ref=send2.at[b, a], dst_ref=recv2.at[b, a_own],
                send_sem=s2_sem.at[b, a], recv_sem=r2_sem.at[b, a_own],
                device_id=(ty * 4 + zh * 2 + core, tx * 4 + z), device_id_type=MESH,
            )
            c.start()
            pending.append(c)
    for t in turns:
        b = (b_own + t) % 4
        part = keep2[b, a_own]
        for u in (1, 3, 2):
            a = (a_own + u) % 4
            pltpu.make_async_remote_copy(
                src_ref=send2.at[b, a], dst_ref=recv2.at[b, a],
                send_sem=s2_sem.at[b, a], recv_sem=r2_sem.at[b, a],
                device_id=(dp, pool), device_id_type=MESH,
            ).wait_recv()
            part = part + recv2[b, a].astype(jnp.float32)
        if t:
            send3[b] = part.astype(send3.dtype)
            ty = y * (1 - core) + b * core
            tx = b * (1 - core) + x * core
            c = pltpu.make_async_remote_copy(
                src_ref=send3.at[b], dst_ref=recv3.at[b_own],
                send_sem=s3_sem.at[b], recv_sem=r3_sem.at[b_own],
                device_id=(ty * 4 + zh * 2 + core, tx * 4 + z), device_id_type=MESH,
            )
            c.start()
            pending.append(c)
    for t in (1, 3, 2):
        b = (b_own + t) % 4
        pltpu.make_async_remote_copy(
            src_ref=send3.at[b], dst_ref=recv3.at[b],
            send_sem=s3_sem.at[b], recv_sem=r3_sem.at[b],
            device_id=(dp, pool), device_id_type=MESH,
        ).wait_recv()
        part = part + recv3[b].astype(jnp.float32)
    for q in range(8):
        send4[q] = part[q * 8:(q + 1) * 8]
    zz = zh * 4 + z
    for t in (4, 3, 5, 2, 6, 1, 7):
        q = (zz + t) % 8
        c = pltpu.make_async_remote_copy(
            src_ref=send4.at[q], dst_ref=recv4.at[zz],
            send_sem=s4_sem.at[q], recv_sem=r4_sem.at[zz],
            device_id=(y * 4 + (q // 4) * 2 + core, x * 4 + q % 4), device_id_type=MESH,
        )
        c.start()
        pending.append(c)
    result = send4[zz]
    for t in (1, 7, 2, 6, 3, 5, 4):
        q = (zz + t) % 8
        pltpu.make_async_remote_copy(
            src_ref=send4.at[q], dst_ref=recv4.at[q],
            send_sem=s4_sem.at[q], recv_sem=r4_sem.at[q],
            device_id=(dp, pool), device_id_type=MESH,
        ).wait_recv()
        result = result + recv4[q]
    out_ref[...] = result
    for c in pending:
        c.wait_send()


def per_device(feats, tower_w, partners, popularity_buckets, row_counts):
    f32, bf16, i32 = jnp.float32, jnp.bfloat16, jnp.int32
    vmem = pltpu.VMEM
    dma = pltpu.SemaphoreType.DMA
    return pl.pallas_call(
        kernel,
        out_shape=pltpu.VMEM((8, DE), f32),
        in_specs=[pl.BlockSpec(memory_space=pl.ANY)] * 5,
        out_specs=pl.BlockSpec(memory_space=pltpu.VMEM),
        scratch_shapes=[
            vmem((ROWS, DIN), bf16),
            vmem((DIN, DE), bf16),
            vmem((1, ROWS), i32),
            vmem((1, ROWS), i32),
            pltpu.SMEM((16, 16), i32),
            vmem((2, 1024, ROWS), bf16),
            vmem((16, ROWS, DE), bf16),
            vmem((16, ROWS, ROWS), f32),
            vmem((16, ROWS, ROWS), f32),
            vmem((16, 2, ROWS), f32),
            vmem((16, 1, ROWS), f32),
            vmem((ROWS, DE), f32),
            vmem((ROWS, 128), f32),
            vmem((ROWS, 128), f32),
            vmem((ROWS, 128), f32),
            vmem((ROWS, 128), f32),
            vmem((ROWS, 128), f32),
            vmem((ROWS, DE), f32),
            vmem((4, 256, DE), bf16),
            vmem((4, 256, DE), bf16),
            vmem((4, 4, 64, DE), f32),
            vmem((4, 4, 64, DE), bf16),
            vmem((4, 4, 64, DE), bf16),
            vmem((4, 64, DE), f32),
            vmem((4, 64, DE), f32),
            vmem((8, 8, DE), f32),
            vmem((8, 8, DE), f32),
            dma((KC, 2)),
            dma((3,)),
            dma((16,)),
            dma((16,)),
            dma((32,)),
            dma((16, 2)),
            dma((16,)),
            dma((16,)),
            dma((4,)),
            dma((4,)),
            dma((4, 4)),
            dma((4, 4)),
            dma((4,)),
            dma((4,)),
            dma((8,)),
            dma((8,)),
        ],
        compiler_params=pltpu.CompilerParams(collective_id=0, has_side_effects=True),
    )(feats, tower_w, partners.reshape(1, ROWS), popularity_buckets.reshape(1, ROWS), row_counts)


def solution(mesh):
    return jax.shard_map(
        per_device,
        mesh=mesh,
        in_specs=(P(("dp", "pool"), None), P(), P(("dp", "pool")), P(("dp", "pool")), P()),
        out_specs=P(("dp", "pool"), None),
        check_vma=False,
    )
```

time: 62.1 us -> 56.1 us (0.903); the launches traced: 61.4 us -> 56 us
  Pallas kernels: 60.1 us -> 55.4 us
  local copies, waits for them, and re-layouts: 1.3 us -> 0.6 us
    pallas_call x1, Pallas kernels: 60.1 us -> 55.4 us  [per_device(): pl.pallas_call(kernel, out_shape=pltpu.VMEM((8, DE), f32), in_specs=[pl.B...]
    unnamed x1, local copies, waits for them, and re-layouts: 1.3 us -> 0.6 us
where the time goes in v2:
time: 56.1 us; the launch traced here: 56 us
  Pallas kernels  55.4 us (99%)
  local copies, waits for them, and re-layouts  0.6 us (1%)
    pallas_call x1, Pallas kernels, per_device(): pl.pallas_call(kernel, out_shape=pltpu.VMEM((8, DE), f32), in_specs=[pl.B...  55.4 us

profile of v2, /device:TPU:6, one launch (start us, length us, event | category | flops | bytes accessed | tf_op | source)
XLA Modules:
  0.0 56.0 jit_solution(16396029558068675884)
XLA Ops:
  0.0 55.4 %shard_map.55 = f32[8,256]{1,0:T(8,128)S(1)} custom-call(bf16[256,2048]{1,0:T(8,128)(2,1)} %feats_hbm.1, bf16[2048,256]{1,0:T(8,128)(2,1)} %w_hbm.1, s32[1,256]{1,0:T(1,128)} %bitcast.2, s32[1,256]{1,0:T(1,128)} %bitcast.3, s32[16,16]{1,0:T(8,128)} %counts_hbm.1), custom_call_target="tpu_custom_call" | custom-call | tf_op jit(solution)/shard_map/pallas_call | solution.py:388
  55.4 0.6 %copy.7 = f32[8,256]{1,0:T(8,128)} copy(f32[8,256]{1,0:T(8,128)S(1)} %shard_map.55) | data formatting | bytes 16384

commit v3 on v2

--- a/solution.py
+++ b/solution.py
@@ -130,13 +130,37 @@
     right = (x + 1) % 4
     left = (x + 3) % 4
     far = (x + 2) % 4
+    middle = z % 2 + z // 2 == 1
     count = iter(range(64))
-    for h in (0, 1):
-        send(pool, h, right * 4 + z, next(count))
-        send(pool, 1 - h, left * 4 + z, next(count))
-    for c in (1, 2, 3):
-        for h in (0, 1):
-            send(pool, h, x * 4 + zs[c], next(count))
+    inner = []
+
+    def to_right(slot, h):
+        send(slot, h, right * 4 + z, next(count))
+
+    def to_left(slot, h):
+        send(slot, h, left * 4 + z, next(count))
+
+    def to_z(slot, h, c):
+        send(slot, h, x * 4 + zs[c], next(count))
+
+    def to_z_from_middle(slot, h, c):
+        n = next(count)
+        cp = pltpu.make_async_remote_copy(
+            src_ref=e_all.at[slot, rows_of(h)], dst_ref=e_all.at[slot, rows_of(h)],
+            send_sem=e_ssem.at[n], recv_sem=e_rsem.at[slot, h],
+            device_id=(dp, x * 4 + zs[c]), device_id_type=MESH,
+        )
+        inner.append(cp)
+        pl.when(middle)(cp.start)
+
+    for h in (0, 1):
+        to_right(pool, h)
+        to_left(pool, 1 - h)
+        to_z(pool, h, 1)
+    for h in (0, 1):
+        to_z(pool, h, 2)
+    for h in (0, 1):
+        to_z_from_middle(pool, h, 3)
     for k in range(1, 16):
         c = pltpu.make_async_remote_copy(
             src_ref=meta.at[pool], dst_ref=meta.at[pool],
@@ -182,41 +206,68 @@
 
     transposes(0, 8)
 
-    for c in range(4):
-        if c < 3:
-            nslot = x * 4 + zs[c + 1]
-            for h in (0, 1):
-                arrive(nslot, h)
-                send(nslot, h, right * 4 + z, next(count))
-                send(nslot, h, left * 4 + z, next(count))
-        ls = left * 4 + zs[c]
-        rs = right * 4 + zs[c]
-        arrive(ls, 0)
-        send(ls, 0, right * 4 + z, next(count))
-        arrive(rs, 1)
-        send(rs, 1, left * 4 + z, next(count))
-        if c == 0:
-            transposes(8, 16)
-        if c < 3:
-            meta_arrive(nslot)
-            scores(nslot)
-        arrive(ls, 1)
-        meta_arrive(ls)
-        scores(ls)
-        arrive(rs, 0)
-        meta_arrive(rs)
-        scores(rs)
-        if c > 0:
-            fs = far * 4 + zs[c - 1]
-            arrive(fs, 0)
-            arrive(fs, 1)
-            meta_arrive(fs)
-            scores(fs)
-    fs = far * 4 + zs[3]
-    arrive(fs, 0)
-    arrive(fs, 1)
-    meta_arrive(fs)
-    scores(fs)
+    def member(dx, c):
+        return ((x + dx) % 4) * 4 + zs[c]
+
+    def take(slot):
+        meta_arrive(slot)
+        scores(slot)
+
+    def turn(c):
+        arrive(member(3, c), 0)
+        to_right(member(3, c), 0)
+        arrive(member(1, c), 1)
+        to_left(member(1, c), 1)
+
+    def spread(c):
+        for h in (0, 1):
+            arrive(member(0, c), h)
+            to_right(member(0, c), h)
+            to_left(member(0, c), h)
+            if c == 2:
+                to_z_from_middle(member(0, c), h, 1)
+
+    def rest(c):
+        arrive(member(3, c), 1)
+        take(member(3, c))
+        arrive(member(1, c), 0)
+        take(member(1, c))
+
+    turn(0)
+    spread(1)
+    transposes(8, 16)
+    take(member(0, 1))
+    rest(0)
+    for h in (0, 1):
+        arrive(member(2, 0), h)
+        to_z(member(2, 0), h, 1)
+        to_z(member(2, 0), h, 3)
+    take(member(2, 0))
+    spread(2)
+    take(member(0, 2))
+    for h in (0, 1):
+        arrive(member(3, 1), h)
+        arrive(member(1, 1), h)
+    take(member(3, 1))
+    take(member(1, 1))
+    turn(2)
+    spread(3)
+    take(member(0, 3))
+    rest(2)
+    arrive(member(2, 1), 0)
+    arrive(member(2, 1), 1)
+    take(member(2, 1))
+    arrive(member(2, 2), 0)
+    arrive(member(2, 2), 1)
+    take(member(2, 2))
+    arrive(member(2, 3), 0)
+    arrive(member(2, 3), 1)
+    take(member(2, 3))
+    for h in (0, 1):
+        arrive(member(3, 3), h)
+        arrive(member(1, 3), h)
+    take(member(3, 3))
+    take(member(1, 3))
 
     order = [
         [(2, 3), (2, 2), (2, 1), (3, 3)],
@@ -224,9 +275,6 @@
         [(3, 1), (1, 1), (0, 3), (0, 2)],
         [(3, 0), (1, 0), (0, 1), (0, 0)],
     ]
-
-    def member(dx, c):
-        return ((x + dx) % 4) * 4 + zs[c]
 
     total = jnp.broadcast_to(jnp.sum(tot_s[...], axis=1, keepdims=True), (ROWS, 128))
     recip_own = own_valid[...] / total
@@ -377,6 +425,8 @@
         ).wait_recv()
         result = result + recv4[q]
     out_ref[...] = result
+    for c in inner:
+        pl.when(middle)(c.wait_send)
     for c in pending:
         c.wait_send()
 
@@ -422,7 +472,7 @@
             dma((3,)),
             dma((16,)),
             dma((16,)),
-            dma((32,)),
+            dma((40,)),
             dma((16, 2)),
             dma((16,)),
             dma((16,)),

time: 56.1 us -> 53.8 us (0.959)
  Pallas kernels: 55.4 us -> 53 us
    pallas_call x1, Pallas kernels: 55.4 us -> 53 us  [per_device(): pl.pallas_call(kernel, out_shape=pltpu.VMEM((8, DE), f32), in_specs=[pl.B...]
where the time goes in v3:
time: 53.8 us; the launch traced here: 53.6 us
  Pallas kernels  53 us (99%)
  local copies, waits for them, and re-layouts  0.6 us (1%)
    pallas_call x1, Pallas kernels, per_device(): pl.pallas_call(kernel, out_shape=pltpu.VMEM((8, DE), f32), in_specs=[pl.B...  53 us

profile of v3, /device:TPU:6, one launch (start us, length us, event | category | flops | bytes accessed | tf_op | source)
XLA Modules:
  0.0 53.6 jit_solution(16672195349018286940)
XLA Ops:
  0.0 53.0 %shard_map.55 = f32[8,256]{1,0:T(8,128)S(1)} custom-call(bf16[256,2048]{1,0:T(8,128)(2,1)} %feats_hbm.1, bf16[2048,256]{1,0:T(8,128)(2,1)} %w_hbm.1, s32[1,256]{1,0:T(1,128)} %bitcast.2, s32[1,256]{1,0:T(1,128)} %bitcast.3, s32[16,16]{1,0:T(8,128)} %counts_hbm.1), custom_call_target="tpu_custom_call" | custom-call | tf_op jit(solution)/shard_map/pallas_call | solution.py:438
  53.0 0.6 %copy.7 = f32[8,256]{1,0:T(8,128)} copy(f32[8,256]{1,0:T(8,128)S(1)} %shard_map.55) | data formatting | bytes 16384

commit v4 on v3

--- a/solution.py
+++ b/solution.py
@@ -134,24 +134,21 @@
     count = iter(range(64))
     inner = []
 
-    def to_right(slot, h):
-        send(slot, h, right * 4 + z, next(count))
-
-    def to_left(slot, h):
-        send(slot, h, left * 4 + z, next(count))
-
-    def to_z(slot, h, c):
-        send(slot, h, x * 4 + zs[c], next(count))
-
-    def to_z_from_middle(slot, h, c):
-        n = next(count)
-        cp = pltpu.make_async_remote_copy(
+    def copy_to_z(slot, h, c, n):
+        return pltpu.make_async_remote_copy(
             src_ref=e_all.at[slot, rows_of(h)], dst_ref=e_all.at[slot, rows_of(h)],
             send_sem=e_ssem.at[n], recv_sem=e_rsem.at[slot, h],
             device_id=(dp, x * 4 + zs[c]), device_id_type=MESH,
         )
-        inner.append(cp)
-        pl.when(middle)(cp.start)
+
+    def to_right(slot, h):
+        send(slot, h, right * 4 + z, next(count))
+
+    def to_left(slot, h):
+        send(slot, h, left * 4 + z, next(count))
+
+    def to_z(slot, h, c):
+        send(slot, h, x * 4 + zs[c], next(count))
 
     for h in (0, 1):
         to_right(pool, h)
@@ -159,8 +156,6 @@
         to_z(pool, h, 1)
     for h in (0, 1):
         to_z(pool, h, 2)
-    for h in (0, 1):
-        to_z_from_middle(pool, h, 3)
     for k in range(1, 16):
         c = pltpu.make_async_remote_copy(
             src_ref=meta.at[pool], dst_ref=meta.at[pool],
@@ -224,8 +219,6 @@
             arrive(member(0, c), h)
             to_right(member(0, c), h)
             to_left(member(0, c), h)
-            if c == 2:
-                to_z_from_middle(member(0, c), h, 1)
 
     def rest(c):
         arrive(member(3, c), 1)
@@ -235,16 +228,54 @@
 
     turn(0)
     spread(1)
+    second, across = member(0, 2), member(2, 0)
+    to_end = [copy_to_z(second, h, 1, 30 + h) for h in (0, 1)]
+    to_other = [copy_to_z(pool, h, 3, 32 + h) for h in (0, 1)]
+    inner += to_end + to_other
+    second_x = []
+    for h in (0, 1):
+        for side in (right, left):
+            second_x.append(pltpu.make_async_remote_copy(
+                src_ref=e_all.at[second, rows_of(h)], dst_ref=e_all.at[second, rows_of(h)],
+                send_sem=e_ssem.at[34 + len(second_x)], recv_sem=e_rsem.at[second, h],
+                device_id=(dp, side * 4 + z), device_id_type=MESH,
+            ))
+    across_z = [copy_to_z(across, h, c, 38 + 2 * h + c // 2) for h in (0, 1) for c in (1, 3)]
+    pending += second_x + across_z
+
+    def send_second(h, relay):
+        arrive(second, h)
+        if relay:
+            to_end[h].start()
+        second_x[2 * h].start()
+        second_x[2 * h + 1].start()
+
+    def send_across(h):
+        arrive(across, h)
+        across_z[2 * h].start()
+        across_z[2 * h + 1].start()
+
+    @pl.when(middle)
+    def _():
+        for cp in to_other:
+            cp.start()
+        for h in (0, 1):
+            send_second(h, True)
+        for h in (0, 1):
+            send_across(h)
+
+    @pl.when(jnp.logical_not(middle))
+    def _():
+        for h in (0, 1):
+            send_across(h)
+        for h in (0, 1):
+            send_second(h, False)
+
     transposes(8, 16)
     take(member(0, 1))
     rest(0)
-    for h in (0, 1):
-        arrive(member(2, 0), h)
-        to_z(member(2, 0), h, 1)
-        to_z(member(2, 0), h, 3)
-    take(member(2, 0))
-    spread(2)
-    take(member(0, 2))
+    take(across)
+    take(second)
     for h in (0, 1):
         arrive(member(3, 1), h)
         arrive(member(1, 1), h)
@@ -472,7 +503,7 @@
             dma((3,)),
             dma((16,)),
             dma((16,)),
-            dma((40,)),
+            dma((42,)),
             dma((16, 2)),
             dma((16,)),
             dma((16,)),

time: 53.8 us -> 51.4 us (0.955)
  Pallas kernels: 53 us -> 50.6 us
    pallas_call x1, Pallas kernels: 53 us -> 50.6 us  [per_device(): pl.pallas_call(kernel, out_shape=pltpu.VMEM((8, DE), f32), in_specs=[pl.B...]
where the time goes in v4:
time: 51.4 us; the launch traced here: 51.2 us
  Pallas kernels  50.6 us (98%)
  local copies, waits for them, and re-layouts  0.6 us (1%)
    pallas_call x1, Pallas kernels, per_device(): pl.pallas_call(kernel, out_shape=pltpu.VMEM((8, DE), f32), in_specs=[pl.B...  50.6 us

profile of v4, /device:TPU:6, one launch (start us, length us, event | category | flops | bytes accessed | tf_op | source)
XLA Modules:
  0.0 51.2 jit_solution(16735247116362490013)
XLA Ops:
  0.0 50.6 %shard_map.55 = f32[8,256]{1,0:T(8,128)S(1)} custom-call(bf16[256,2048]{1,0:T(8,128)(2,1)} %feats_hbm.1, bf16[2048,256]{1,0:T(8,128)(2,1)} %w_hbm.1, s32[1,256]{1,0:T(1,128)} %bitcast.2, s32[1,256]{1,0:T(1,128)} %bitcast.3, s32[16,16]{1,0:T(8,128)} %counts_hbm.1), custom_call_target="tpu_custom_call" | custom-call | tf_op jit(solution)/shard_map/pallas_call | solution.py:469
  50.6 0.6 %copy.7 = f32[8,256]{1,0:T(8,128)} copy(f32[8,256]{1,0:T(8,128)S(1)} %shard_map.55) | data formatting | bytes 16384

commit v5 on v2

v5 whole, which is shorter than its diff:
```python
import functools

import jax
import jax.numpy as jnp
from jax import lax
from jax.experimental import pallas as pl
from jax.experimental.pallas import tpu as pltpu
from jax.sharding import PartitionSpec as P

MESH = pl.DeviceIdType.MESH
EPS = 1e-06
SCALE = 28.853900817779268
ROWS = 256
HALF = 128
DE = 256
DIN = 2048
KC = 4
KW = DIN // KC


def nt(left, right):
    return lax.dot_general(
        left, right, (((1,), (1,)), ((), ())), preferred_element_type=jnp.float32
    )


def nn(left, right):
    return jnp.dot(left, right, preferred_element_type=jnp.float32)


def kernel(
    feats_hbm, w_hbm, part_hbm, buck_hbm, counts_hbm, out_ref,
    feats_v, w_v, part_v, buck_v, counts_v, feats_t, e_all, a_all, b_all, meta, recips,
    normed_s, inv_s, own_w, own_part, own_valid, tot_s, g_s,
    core_send, core_recv, keep2, send2, recv2, send3, recv3, send4, recv4,
    in_sem, small_sem, out_sem, m_sem, e_sem, r_sem, c_sem, r2_sem, r3_sem, r4_sem,
):
    dp = lax.axis_index("dp")
    pool = lax.axis_index("pool")
    y = dp // 4
    zh = (dp // 2) % 2
    core = dp % 2
    x = pool // 4
    z = pool % 4
    zs = [z, z + 1 - 2 * (z % 2), (z + 2) % 4, 3 - z]
    middle = z % 2 + z // 2 == 1
    right = (x + 1) % 4
    left = (x + 3) % 4

    def member(dx, c):
        return ((x + dx) % 4) * 4 + zs[c]

    S_META, S_COL, S_E, S_MID, S_RECIP, S_CORE, S_TWO, S_THREE, S_FOUR = range(9)

    def remote(src, dst, kind, sem, d, p):
        return pltpu.make_async_remote_copy(
            src_ref=src, dst_ref=dst, send_sem=out_sem.at[kind], recv_sem=sem,
            device_id=(d, p), device_id_type=MESH,
        )

    def landed(ref, sem):
        remote(ref, ref, 0, sem, dp, pool).wait_recv()

    barrier = pltpu.get_barrier_semaphore()

    def greet(d, p):
        pl.semaphore_signal(barrier, inc=1, device_id=(d, p), device_id_type=MESH)

    for k in range(1, 16):
        greet(dp, (pool + k) % 16)
    greet(y * 4 + zh * 2 + (1 - core), pool)
    for k in range(1, 4):
        greet(((y + k) % 4) * 4 + zh * 2 + core, pool)
    for k in range(4):
        greet(y * 4 + (1 - zh) * 2 + core, x * 4 + k)

    for k in range(KC):
        cols = pl.ds(k * KW, KW)
        pltpu.make_async_copy(feats_hbm.at[:, cols], feats_v.at[:, cols], in_sem.at[k]).start()
        pltpu.make_async_copy(w_hbm.at[cols, :], w_v.at[cols, :], in_sem.at[k]).start()
    small = [
        pltpu.make_async_copy(part_hbm, part_v, small_sem.at[0]),
        pltpu.make_async_copy(buck_hbm, buck_v, small_sem.at[1]),
        pltpu.make_async_copy(counts_hbm, counts_v, small_sem.at[2]),
    ]
    for c in small:
        c.start()

    projected = None
    for k in range(KC):
        both = pl.ds(0, 2 * KW)
        pltpu.make_async_copy(w_hbm.at[both, :], w_v.at[both, :], in_sem.at[k]).wait()
        cols = pl.ds(k * KW, KW)
        term = nn(feats_v[:, cols], w_v[cols, :])
        projected = term if projected is None else projected + term
    inv_norm = lax.rsqrt(jnp.sum(projected * projected, axis=1, keepdims=True) + EPS)
    normed = projected * inv_norm
    normed_s[...] = normed
    inv_s[...] = jnp.broadcast_to(inv_norm, (ROWS, 128))
    e_all[pool] = normed.astype(jnp.bfloat16)

    for c in small:
        c.wait()
    cnt = counts_v[dp, pool]
    lane = lax.broadcasted_iota(jnp.int32, (1, ROWS), 1)
    valid = lane < cnt
    part_l = jnp.where(valid, part_v[...], -1).astype(jnp.float32)
    w_l = jnp.where(valid, jnp.exp((buck_v[...].astype(jnp.float32) + 0.5) * 0.25), 0.0)
    meta[pool, 0:1, :] = part_l
    meta[pool, 1:2, :] = w_l

    pl.semaphore_wait(barrier, 23)

    for c in (1, 2, 3):
        remote(meta.at[pool], meta.at[pool], S_META, m_sem.at[0], dp, member(0, c)).start()

    def rows_of(h):
        return pl.ds(h * HALF, HALF)

    def sem_of(dx, c, h):
        if dx == 0:
            return e_sem.at[2 * (c - 1) + h]
        if dx == 2:
            return e_sem.at[6 + h] if c == 0 else e_sem.at[15 + c]
        if c % 2:
            return e_sem.at[14 + c // 2]
        onward = h == (0 if dx == 3 else 1)
        return e_sem.at[(8 if c == 0 else 11) + (1 if not onward else 0 if dx == 3 else 2)]

    def copy(dx, c, h, side, kind=S_E):
        slot = member(dx, c)
        half = e_all.at[slot, rows_of(h)]
        if side == "right":
            return remote(half, half, kind, sem_of((dx + 3) % 4, c, h), dp, right * 4 + z)
        if side == "left":
            return remote(half, half, kind, sem_of((dx + 1) % 4, c, h), dp, left * 4 + z)
        return remote(half, half, kind, sem_of(dx, c ^ side, h), dp, x * 4 + zs[side])

    def arrive(dx, c, h):
        landed(e_all.at[member(dx, c), rows_of(h)], sem_of(dx, c, h))

    for h in (0, 1):
        copy(0, 0, h, "right").start()
        copy(0, 0, 1 - h, "left").start()
        copy(0, 0, h, 1).start()

    @pl.when(jnp.logical_not(middle))
    def _():
        for h in (0, 1):
            copy(0, 0, h, 2).start()

    own_part[...] = jnp.broadcast_to(part_l, (128, ROWS)).T
    own_w[...] = jnp.broadcast_to(w_l, (128, ROWS)).T
    own_valid[...] = jnp.broadcast_to(jnp.where(valid, 1.0, 0.0), (128, ROWS)).T

    def wide(v):
        return jnp.concatenate([v, v], axis=1)

    def scores(dx, c):
        slot = member(dx, c)
        s = nt(e_all[pool], e_all[slot])
        e = jnp.exp2(s * SCALE)
        if (dx, c) == (0, 0):
            ri = lax.broadcasted_iota(jnp.int32, (ROWS, ROWS), 0)
            ci = lax.broadcasted_iota(jnp.int32, (ROWS, ROWS), 1)
            e = jnp.where(ri == ci, 0.0, e)
        b_all[slot] = e * wide(own_w[...])
        t = e * meta[slot, 1:2, :]
        a_all[slot] = t
        t = t[:, :128] + t[:, 128:]
        if (dx, c) == (0, 0):
            tot_s[...] = t
        else:
            tot_s[...] += t

    scores(0, 0)

    def transposes(lo, hi):
        for m in range(lo, hi):
            my, mz, mc = m // 4, (m // 2) % 2, m % 2
            t = feats_v[:, m * 128:(m + 1) * 128].T
            which = (mc + core) % 2
            for mx in range(4):
                at = (my * (2 + 6 * mc) + mx * (8 - 6 * mc) + mz) * 32
                feats_t[which, at:at + 32, :] = t[mx * 32:(mx + 1) * 32]

    transposes(0, 16)

    @pl.when(middle)
    def _():
        for h in (0, 1):
            copy(0, 0, h, 2).start()

    def spread(c):
        for h in (0, 1):
            arrive(0, c, h)
            copy(0, c, h, "right").start()
            copy(0, c, h, "left").start()

    def rest(c):
        landed(e_all.at[member(3, c)], sem_of(3, c, 1))
        scores(3, c)
        scores(1, c)

    arrive(3, 0, 0)
    copy(3, 0, 0, "right").start()

    arrive(1, 0, 1)
    copy(1, 0, 1, "left").start()
    column = meta.at[pl.ds(x * 4, 4)]
    landed(meta.at[0:3], m_sem.at[0])
    for dx in (1, 3, 2):
        remote(column, column, S_COL, m_sem.at[1], dp, member(dx, 0)).start()
    spread(1)

    def send_second(relay):
        for h in (0, 1):
            arrive(0, 2, h)
            if relay:
                copy(0, 2, h, 1, S_MID).start()
            copy(0, 2, h, "right").start()
            copy(0, 2, h, "left").start()

    def send_across():
        for h in (0, 1):
            arrive(2, 0, h)
            copy(2, 0, h, 1).start()
            copy(2, 0, h, 3).start()

    @pl.when(middle)
    def _():
        for h in (0, 1):
            copy(0, 0, h, 3, S_MID).start()
        send_second(True)
        send_across()

    @pl.when(jnp.logical_not(middle))
    def _():
        send_across()
        send_second(False)

    scores(0, 1)
    landed(meta.at[0:12], m_sem.at[1])
    rest(0)
    scores(2, 0)
    scores(0, 2)
    landed(e_all.at[0:2], sem_of(3, 1, 0))
    scores(3, 1)
    scores(1, 1)
    arrive(3, 2, 0)
    copy(3, 2, 0, "right").start()
    arrive(1, 2, 1)
    copy(1, 2, 1, "left").start()
    spread(3)
    scores(0, 3)
    rest(2)
    for c in (1, 2, 3):
        landed(e_all.at[member(2, c)], sem_of(2, c, 0))
        scores(2, c)
    landed(e_all.at[0:2], sem_of(3, 3, 0))
    scores(3, 3)
    scores(1, 3)

    near = [
        [(0, 0), (0, 1), (1, 0), (3, 0)],
        [(0, 2), (0, 3), (1, 1), (3, 1)],
        [(2, 0), (1, 2), (3, 2), (1, 3), (3, 3)],
        [(2, 1), (2, 2), (2, 3)],
    ]
    total = jnp.broadcast_to(jnp.sum(tot_s[...], axis=1, keepdims=True), (ROWS, 128))
    recip_own = own_valid[...] / total
    recips[pool] = recip_own.T[0:1, :]
    for n, group in reversed(list(enumerate(near))):
        for dx, c in reversed(group):
            if (dx, c) != (0, 0):
                remote(recips.at[pool], recips.at[pool], S_RECIP, r_sem.at[n], dp, member(dx, c)).start()

    tot_s[...] = recip_own
    g_s[...] = jnp.zeros_like(g_s)
    lane_f = lax.broadcasted_iota(jnp.int32, (1, ROWS), 1).astype(jnp.float32)

    def row_term(i, carry):
        acc = None
        for j in range(4):
            s = i * 4 + j
            hit = wide(own_part[...]) == lane_f + (s * ROWS).astype(jnp.float32)
            coef = a_all[s] * wide(tot_s[...])
            coef = jnp.where(hit, coef - 1.0, coef).astype(jnp.bfloat16)
            term = nn(coef, e_all[s])
            acc = term if acc is None else acc + term
        g_s[...] += acc
        return carry

    lax.fori_loop(0, 4, row_term, 0)

    mine = lax.broadcasted_iota(jnp.int32, (ROWS, 128), 0).astype(jnp.float32) + (pool * ROWS).astype(jnp.float32)
    own_part[...] = mine
    for n, group in enumerate(near):
        landed(recips.at[0:len(group) - (n == 0)], r_sem.at[n])
        acc = None
        for dx, c in group:
            s = member(dx, c)
            hit = wide(own_part[...]) == meta[s, 0:1, :]
            coef = b_all[s] * recips[s]
            coef = jnp.where(hit, coef - 1.0, coef).astype(jnp.bfloat16)
            term = nn(coef, e_all[s])
            acc = term if acc is None else acc + term
        g_s[...] += acc

    g = g_s[...]
    nrm = normed_s[...]
    g = (g - nrm * jnp.sum(nrm * g, axis=1, keepdims=True)) * wide(inv_s[...])
    gp = g.astype(jnp.bfloat16)

    a_own = y * (1 - core) + x * core
    b_own = x * (1 - core) + y * core
    turns = (2, 1, 3, 0)
    for t in turns:
        b = (a_own + t) % 4
        core_send[b] = nn(feats_t[1, pl.ds(pl.multiple_of(b * 256, 256), 256), :], gp).astype(core_send.dtype)
        remote(
            core_send.at[b], core_recv.at[b], S_CORE, c_sem.at[b], y * 4 + zh * 2 + (1 - core), pool
        ).start()
    for t in turns:
        b = (b_own + t) % 4
        own = nn(feats_t[0, pl.ds(pl.multiple_of(b * 256, 256), 256), :], gp)
        landed(core_recv.at[b], c_sem.at[b])
        own = own + core_recv[b].astype(jnp.float32)
        for q in range(4):
            keep2[b, q] = own[q * 64:(q + 1) * 64]
            send2[b, q] = own[q * 64:(q + 1) * 64].astype(send2.dtype)
        for u in (2, 1, 3):
            a = (a_own + u) % 4
            ty = a * (1 - core) + y * core
            tx = x * (1 - core) + a * core
            remote(
                send2.at[b, a], recv2.at[b, a_own], S_TWO, r2_sem.at[b], ty * 4 + zh * 2 + core, tx * 4 + z
            ).start()
    for t in turns:
        b = (b_own + t) % 4
        part = keep2[b, a_own]
        landed(recv2.at[b, 0:3], r2_sem.at[b])
        for u in (1, 3, 2):
            part = part + recv2[b, (a_own + u) % 4].astype(jnp.float32)
        if t:
            send3[b] = part.astype(send3.dtype)
            ty = y * (1 - core) + b * core
            tx = b * (1 - core) + x * core
            remote(
                send3.at[b], recv3.at[b_own], S_THREE, r3_sem.at[0], ty * 4 + zh * 2 + core, tx * 4 + z
            ).start()
    landed(recv3.at[0:3], r3_sem.at[0])
    for t in (1, 3, 2):
        part = part + recv3[(b_own + t) % 4].astype(jnp.float32)
    for q in range(8):
        send4[q] = part[q * 8:(q + 1) * 8]
    zz = zh * 4 + z
    for t in (4, 3, 5, 2, 6, 1, 7):
        q = (zz + t) % 8
        remote(
            send4.at[q], recv4.at[zz], S_FOUR, r4_sem.at[0], y * 4 + (q // 4) * 2 + core, x * 4 + q % 4
        ).start()
    result = send4[zz]
    landed(recv4.at[0:7], r4_sem.at[0])
    for t in (1, 7, 2, 6, 3, 5, 4):
        result = result + recv4[(zz + t) % 8]
    out_ref[...] = result

    def sent(ref, kind):
        remote(ref, ref, kind, r4_sem.at[0], dp, pool).wait_send()

    sent(meta.at[0:3], S_META)
    sent(meta.at[0:12], S_COL)
    sent(e_all.at[0:14], S_E)
    pl.when(middle)(lambda: sent(e_all.at[0:2], S_MID))
    sent(recips.at[0:15], S_RECIP)
    sent(core_send, S_CORE)
    sent(send2.at[0:3], S_TWO)
    sent(send3.at[0:3], S_THREE)
    sent(send4.at[0:7], S_FOUR)


def per_device(feats, tower_w, partners, popularity_buckets, row_counts):
    f32, bf16, i32 = jnp.float32, jnp.bfloat16, jnp.int32
    vmem = pltpu.VMEM
    dma = pltpu.SemaphoreType.DMA
    return pl.pallas_call(
        kernel,
        out_shape=pltpu.VMEM((8, DE), f32),
        in_specs=[pl.BlockSpec(memory_space=pl.ANY)] * 5,
        out_specs=pl.BlockSpec(memory_space=pltpu.VMEM),
        scratch_shapes=[
            vmem((ROWS, DIN), bf16),
            vmem((DIN, DE), bf16),
            vmem((1, ROWS), i32),
            vmem((1, ROWS), i32),
            pltpu.SMEM((16, 16), i32),
            vmem((2, 1024, ROWS), bf16),
            vmem((16, ROWS, DE), bf16),
            vmem((16, ROWS, ROWS), f32),
            vmem((16, ROWS, ROWS), f32),
            vmem((16, 2, ROWS), f32),
            vmem((16, 1, ROWS), f32),
            vmem((ROWS, DE), f32),
            vmem((ROWS, 128), f32),
            vmem((ROWS, 128), f32),
            vmem((ROWS, 128), f32),
            vmem((ROWS, 128), f32),
            vmem((ROWS, 128), f32),
            vmem((ROWS, DE), f32),
            vmem((4, 256, DE), bf16),
            vmem((4, 256, DE), bf16),
            vmem((4, 4, 64, DE), f32),
            vmem((4, 4, 64, DE), bf16),
            vmem((4, 4, 64, DE), bf16),
            vmem((4, 64, DE), f32),
            vmem((4, 64, DE), f32),
            vmem((8, 8, DE), f32),
            vmem((8, 8, DE), f32),
            dma((KC,)),
            dma((3,)),
            dma((9,)),
            dma((2,)),
            dma((19,)),
            dma((4,)),
            dma((4,)),
            dma((4,)),
            dma((1,)),
            dma((1,)),
        ],
        compiler_params=pltpu.CompilerParams(collective_id=0, has_side_effects=True),
    )(feats, tower_w, partners.reshape(1, ROWS), popularity_buckets.reshape(1, ROWS), row_counts)


def solution(mesh):
    return jax.shard_map(
        per_device,
        mesh=mesh,
        in_specs=(P(("dp", "pool"), None), P(), P(("dp", "pool")), P(("dp", "pool")), P()),
        out_specs=P(("dp", "pool"), None),
        check_vma=False,
    )
```

time: 56.1 us -> 49.2 us (0.88)
  Pallas kernels: 55.4 us -> 48.5 us
    pallas_call x1, Pallas kernels: 55.4 us -> 48.5 us  [per_device(): pl.pallas_call(kernel, out_shape=pltpu.VMEM((8, DE), f32), in_specs=[pl.B...]
where the time goes in v5:
time: 49.2 us; the launch traced here: 49.1 us
  Pallas kernels  48.5 us (99%)
  local copies, waits for them, and re-layouts  0.6 us (1%)
    pallas_call x1, Pallas kernels, per_device(): pl.pallas_call(kernel, out_shape=pltpu.VMEM((8, DE), f32), in_specs=[pl.B...  48.5 us

profile of v5, /device:TPU:6, one launch (start us, length us, event | category | flops | bytes accessed | tf_op | source)
XLA Modules:
  0.0 49.1 jit_solution(13009483710039913672)
XLA Ops:
  0.0 48.5 %shard_map.55 = f32[8,256]{1,0:T(8,128)S(1)} custom-call(bf16[256,2048]{1,0:T(8,128)(2,1)} %feats_hbm.1, bf16[2048,256]{1,0:T(8,128)(2,1)} %w_hbm.1, s32[1,256]{1,0:T(1,128)} %bitcast.2, s32[1,256]{1,0:T(1,128)} %bitcast.3, s32[16,16]{1,0:T(8,128)} %counts_hbm.1), custom_call_target="tpu_custom_call" | custom-call | tf_op jit(solution)/shard_map/pallas_call | solution.py:387
  48.5 0.6 %copy.7 = f32[8,256]{1,0:T(8,128)} copy(f32[8,256]{1,0:T(8,128)S(1)} %shard_map.55) | data formatting | bytes 16384

commit v6 on v5

--- a/solution.py
+++ b/solution.py
@@ -31,9 +31,9 @@
 def kernel(
     feats_hbm, w_hbm, part_hbm, buck_hbm, counts_hbm, out_ref,
     feats_v, w_v, part_v, buck_v, counts_v, feats_t, e_all, a_all, b_all, meta, recips,
-    normed_s, inv_s, own_w, own_part, own_valid, tot_s, g_s,
+    normed_s, inv_s, own_w, own_part, own_valid, tot_s, g_s, size,
     core_send, core_recv, keep2, send2, recv2, send3, recv3, send4, recv4,
-    in_sem, small_sem, out_sem, m_sem, e_sem, r_sem, c_sem, r2_sem, r3_sem, r4_sem,
+    in_sem, small_sem, out_sem, e_sem, r_sem, c_sem, r2_sem, r3_sem, r4_sem,
 ):
     dp = lax.axis_index("dp")
     pool = lax.axis_index("pool")
@@ -50,7 +50,7 @@
     def member(dx, c):
         return ((x + dx) % 4) * 4 + zs[c]
 
-    S_META, S_COL, S_E, S_MID, S_RECIP, S_CORE, S_TWO, S_THREE, S_FOUR = range(9)
+    S_META, S_MIDMETA, S_E, S_MID, S_RECIP, S_CORE, S_TWO, S_THREE, S_FOUR = range(9)
 
     def remote(src, dst, kind, sem, d, p):
         return pltpu.make_async_remote_copy(
@@ -66,13 +66,14 @@
     def greet(d, p):
         pl.semaphore_signal(barrier, inc=1, device_id=(d, p), device_id_type=MESH)
 
-    for k in range(1, 16):
-        greet(dp, (pool + k) % 16)
+    zz = zh * 4 + z
+    for k in (2, 6, 1, 7):
+        q = (zz + k) % 8
+        greet(y * 4 + (q // 4) * 2 + core, x * 4 + q % 4)
+    for k in (2, 1, 3):
+        greet(dp, ((x + k) % 4) * 4 + z)
+        greet(((y + k) % 4) * 4 + zh * 2 + core, pool)
     greet(y * 4 + zh * 2 + (1 - core), pool)
-    for k in range(1, 4):
-        greet(((y + k) % 4) * 4 + zh * 2 + core, pool)
-    for k in range(4):
-        greet(y * 4 + (1 - zh) * 2 + core, x * 4 + k)
 
     for k in range(KC):
         cols = pl.ds(k * KW, KW)
@@ -109,10 +110,7 @@
     meta[pool, 0:1, :] = part_l
     meta[pool, 1:2, :] = w_l
 
-    pl.semaphore_wait(barrier, 23)
-
-    for c in (1, 2, 3):
-        remote(meta.at[pool], meta.at[pool], S_META, m_sem.at[0], dp, member(0, c)).start()
+    pl.semaphore_wait(barrier, 11)
 
     def rows_of(h):
         return pl.ds(h * HALF, HALF)
@@ -127,27 +125,33 @@
         onward = h == (0 if dx == 3 else 1)
         return e_sem.at[(8 if c == 0 else 11) + (1 if not onward else 0 if dx == 3 else 2)]
 
-    def copy(dx, c, h, side, kind=S_E):
+    def go(dx, c, h, side, middle_only=False):
         slot = member(dx, c)
+        if side == "right":
+            sem, target = sem_of((dx + 3) % 4, c, h), right * 4 + z
+        elif side == "left":
+            sem, target = sem_of((dx + 1) % 4, c, h), left * 4 + z
+        else:
+            sem, target = sem_of(dx, c ^ side, h), x * 4 + zs[side]
         half = e_all.at[slot, rows_of(h)]
-        if side == "right":
-            return remote(half, half, kind, sem_of((dx + 3) % 4, c, h), dp, right * 4 + z)
-        if side == "left":
-            return remote(half, half, kind, sem_of((dx + 1) % 4, c, h), dp, left * 4 + z)
-        return remote(half, half, kind, sem_of(dx, c ^ side, h), dp, x * 4 + zs[side])
+        remote(half, half, S_MID if middle_only else S_E, sem, dp, target).start()
+        if h:
+            remote(
+                meta.at[slot], meta.at[slot], S_MIDMETA if middle_only else S_META, sem, dp, target
+            ).start()
 
     def arrive(dx, c, h):
-        landed(e_all.at[member(dx, c), rows_of(h)], sem_of(dx, c, h))
+        landed(size.at[0:32 + h], sem_of(dx, c, h))
 
     for h in (0, 1):
-        copy(0, 0, h, "right").start()
-        copy(0, 0, 1 - h, "left").start()
-        copy(0, 0, h, 1).start()
+        go(0, 0, h, "right")
+        go(0, 0, 1 - h, "left")
+        go(0, 0, h, 1)
 
     @pl.when(jnp.logical_not(middle))
     def _():
         for h in (0, 1):
-            copy(0, 0, h, 2).start()
+            go(0, 0, h, 2)
 
     own_part[...] = jnp.broadcast_to(part_l, (128, ROWS)).T
     own_w[...] = jnp.broadcast_to(w_l, (128, ROWS)).T
@@ -189,48 +193,44 @@
     @pl.when(middle)
     def _():
         for h in (0, 1):
-            copy(0, 0, h, 2).start()
+            go(0, 0, h, 2)
 
     def spread(c):
         for h in (0, 1):
             arrive(0, c, h)
-            copy(0, c, h, "right").start()
-            copy(0, c, h, "left").start()
+            go(0, c, h, "right")
+            go(0, c, h, "left")
 
     def rest(c):
-        landed(e_all.at[member(3, c)], sem_of(3, c, 1))
+        landed(size.at[0:65], sem_of(3, c, 1))
         scores(3, c)
         scores(1, c)
 
     arrive(3, 0, 0)
-    copy(3, 0, 0, "right").start()
+    go(3, 0, 0, "right")
 
     arrive(1, 0, 1)
-    copy(1, 0, 1, "left").start()
-    column = meta.at[pl.ds(x * 4, 4)]
-    landed(meta.at[0:3], m_sem.at[0])
-    for dx in (1, 3, 2):
-        remote(column, column, S_COL, m_sem.at[1], dp, member(dx, 0)).start()
+    go(1, 0, 1, "left")
     spread(1)
 
     def send_second(relay):
         for h in (0, 1):
             arrive(0, 2, h)
             if relay:
-                copy(0, 2, h, 1, S_MID).start()
-            copy(0, 2, h, "right").start()
-            copy(0, 2, h, "left").start()
+                go(0, 2, h, 1, True)
+            go(0, 2, h, "right")
+            go(0, 2, h, "left")
 
     def send_across():
         for h in (0, 1):
             arrive(2, 0, h)
-            copy(2, 0, h, 1).start()
-            copy(2, 0, h, 3).start()
+            go(2, 0, h, 1)
+            go(2, 0, h, 3)
 
     @pl.when(middle)
     def _():
         for h in (0, 1):
-            copy(0, 0, h, 3, S_MID).start()
+            go(0, 0, h, 3, True)
         send_second(True)
         send_across()
 
@@ -240,32 +240,31 @@
         send_second(False)
 
     scores(0, 1)
-    landed(meta.at[0:12], m_sem.at[1])
     rest(0)
     scores(2, 0)
     scores(0, 2)
-    landed(e_all.at[0:2], sem_of(3, 1, 0))
+    landed(size.at[0:130], sem_of(3, 1, 0))
     scores(3, 1)
     scores(1, 1)
     arrive(3, 2, 0)
-    copy(3, 2, 0, "right").start()
+    go(3, 2, 0, "right")
     arrive(1, 2, 1)
-    copy(1, 2, 1, "left").start()
+    go(1, 2, 1, "left")
     spread(3)
     scores(0, 3)
     rest(2)
     for c in (1, 2, 3):
-        landed(e_all.at[member(2, c)], sem_of(2, c, 0))
+        landed(size.at[0:65], sem_of(2, c, 0))
         scores(2, c)
-    landed(e_all.at[0:2], sem_of(3, 3, 0))
+    landed(size.at[0:130], sem_of(3, 3, 0))
     scores(3, 3)
     scores(1, 3)
 
     near = [
         [(0, 0), (0, 1), (1, 0), (3, 0)],
         [(0, 2), (0, 3), (1, 1), (3, 1)],
-        [(2, 0), (1, 2), (3, 2), (1, 3), (3, 3)],
-        [(2, 1), (2, 2), (2, 3)],
+        [(2, 0), (1, 2), (3, 2), (1, 3), (3, 3), (2, 1)],
+        [(2, 2), (2, 3)],
     ]
     total = jnp.broadcast_to(jnp.sum(tot_s[...], axis=1, keepdims=True), (ROWS, 128))
     recip_own = own_valid[...] / total
@@ -354,7 +353,6 @@
         part = part + recv3[(b_own + t) % 4].astype(jnp.float32)
     for q in range(8):
         send4[q] = part[q * 8:(q + 1) * 8]
-    zz = zh * 4 + z
     for t in (4, 3, 5, 2, 6, 1, 7):
         q = (zz + t) % 8
         remote(
@@ -369,8 +367,8 @@
     def sent(ref, kind):
         remote(ref, ref, kind, r4_sem.at[0], dp, pool).wait_send()
 
-    sent(meta.at[0:3], S_META)
-    sent(meta.at[0:12], S_COL)
+    sent(meta.at[0:14], S_META)
+    pl.when(middle)(lambda: sent(meta.at[0:2], S_MIDMETA))
     sent(e_all.at[0:14], S_E)
     pl.when(middle)(lambda: sent(e_all.at[0:2], S_MID))
     sent(recips.at[0:15], S_RECIP)
@@ -408,19 +406,19 @@
             vmem((ROWS, 128), f32),
             vmem((ROWS, 128), f32),
             vmem((ROWS, DE), f32),
+            vmem((130, 2, ROWS), f32),
             vmem((4, 256, DE), bf16),
             vmem((4, 256, DE), bf16),
             vmem((4, 4, 64, DE), f32),
             vmem((4, 4, 64, DE), bf16),
             vmem((4, 4, 64, DE), bf16),
-            vmem((4, 64, DE), f32),
-            vmem((4, 64, DE), f32),
+            vmem((4, 64, DE), bf16),
+            vmem((4, 64, DE), bf16),
             vmem((8, 8, DE), f32),
             vmem((8, 8, DE), f32),
             dma((KC,)),
             dma((3,)),
             dma((9,)),
-            dma((2,)),
             dma((19,)),
             dma((4,)),
             dma((4,)),

time: 49.2 us -> 48.2 us (0.980)
  Pallas kernels: 48.5 us -> 47.4 us
    pallas_call x1, Pallas kernels: 48.5 us -> 47.4 us  [per_device(): pl.pallas_call(kernel, out_shape=pltpu.VMEM((8, DE), f32), in_specs=[pl.B...]
where the time goes in v6:
time: 48.2 us; the launch traced here: 48 us
  Pallas kernels  47.4 us (98%)
  local copies, waits for them, and re-layouts  0.6 us (1%)
    pallas_call x1, Pallas kernels, per_device(): pl.pallas_call(kernel, out_shape=pltpu.VMEM((8, DE), f32), in_specs=[pl.B...  47.4 us

profile of v6, /device:TPU:6, one launch (start us, length us, event | category | flops | bytes accessed | tf_op | source)
XLA Modules:
  0.0 48.0 jit_solution(706482822661663752)
XLA Ops:
  0.0 47.4 %shard_map.55 = f32[8,256]{1,0:T(8,128)S(1)} custom-call(bf16[256,2048]{1,0:T(8,128)(2,1)} %feats_hbm.1, bf16[2048,256]{1,0:T(8,128)(2,1)} %w_hbm.1, s32[1,256]{1,0:T(1,128)} %bitcast.2, s32[1,256]{1,0:T(1,128)} %bitcast.3, s32[16,16]{1,0:T(8,128)} %counts_hbm.1), custom_call_target="tpu_custom_call" | custom-call | tf_op jit(solution)/shard_map/pallas_call | solution.py:385
  47.4 0.6 %copy.7 = f32[8,256]{1,0:T(8,128)} copy(f32[8,256]{1,0:T(8,128)S(1)} %shard_map.55) | data formatting | bytes 16384

commit v7 on v6

--- a/solution.py
+++ b/solution.py
@@ -192,8 +192,7 @@
 
     @pl.when(middle)
     def _():
-        for h in (0, 1):
-            go(0, 0, h, 2)
+        go(0, 0, 0, 2)
 
     def spread(c):
         for h in (0, 1):
@@ -208,6 +207,10 @@
 
     arrive(3, 0, 0)
     go(3, 0, 0, "right")
+
+    @pl.when(middle)
+    def _():
+        go(0, 0, 1, 2)
 
     arrive(1, 0, 1)
     go(1, 0, 1, "left")
@@ -229,9 +232,9 @@
 
     @pl.when(middle)
     def _():
+        send_second(True)
         for h in (0, 1):
             go(0, 0, h, 3, True)
-        send_second(True)
         send_across()
 
     @pl.when(jnp.logical_not(middle))

time: 48.2 us -> 48 us (level)
  no operation moved by 1% of the time
where the time goes in v7:
time: 48 us; the launch traced here: 47.9 us
  Pallas kernels  47.3 us (99%)
  local copies, waits for them, and re-layouts  0.6 us (1%)
    pallas_call x1, Pallas kernels, per_device(): pl.pallas_call(kernel, out_shape=pltpu.VMEM((8, DE), f32), in_specs=[pl.B...  47.3 us

profile of v7, /device:TPU:6, one launch (start us, length us, event | category | flops | bytes accessed | tf_op | source)
XLA Modules:
  0.0 47.9 jit_solution(4229158492074197459)
XLA Ops:
  0.0 47.3 %shard_map.55 = f32[8,256]{1,0:T(8,128)S(1)} custom-call(bf16[256,2048]{1,0:T(8,128)(2,1)} %feats_hbm.1, bf16[2048,256]{1,0:T(8,128)(2,1)} %w_hbm.1, s32[1,256]{1,0:T(1,128)} %bitcast.2, s32[1,256]{1,0:T(1,128)} %bitcast.3, s32[16,16]{1,0:T(8,128)} %counts_hbm.1), custom_call_target="tpu_custom_call" | custom-call | tf_op jit(solution)/shard_map/pallas_call | solution.py:388
  47.3 0.6 %copy.7 = f32[8,256]{1,0:T(8,128)} copy(f32[8,256]{1,0:T(8,128)S(1)} %shard_map.55) | data formatting | bytes 16384

commit v8 on v7

--- a/solution.py
+++ b/solution.py
@@ -18,14 +18,24 @@
 KW = DIN // KC
 
 
+def by_halves(left, right, contract):
+    return jnp.concatenate(
+        [
+            lax.dot_general(
+                left[at:at + HALF], right, (((1,), (contract,)), ((), ())), preferred_element_type=jnp.float32
+            )
+            for at in range(0, left.shape[0], HALF)
+        ],
+        axis=0,
+    )
+
+
 def nt(left, right):
-    return lax.dot_general(
-        left, right, (((1,), (1,)), ((), ())), preferred_element_type=jnp.float32
-    )
+    return by_halves(left, right, 1)
 
 
 def nn(left, right):
-    return jnp.dot(left, right, preferred_element_type=jnp.float32)
+    return by_halves(left, right, 0)
 
 
 def kernel(
@@ -269,15 +279,15 @@
         [(2, 0), (1, 2), (3, 2), (1, 3), (3, 3), (2, 1)],
         [(2, 2), (2, 3)],
     ]
-    total = jnp.broadcast_to(jnp.sum(tot_s[...], axis=1, keepdims=True), (ROWS, 128))
-    recip_own = own_valid[...] / total
-    recips[pool] = recip_own.T[0:1, :]
+    by_lane = jnp.sum(tot_s[...].T, axis=0, keepdims=True)
+    recips[pool] = jnp.where(meta[pool, 1:2, :] > 0.0, 1.0, 0.0) / by_lane
     for n, group in reversed(list(enumerate(near))):
         for dx, c in reversed(group):
             if (dx, c) != (0, 0):
                 remote(recips.at[pool], recips.at[pool], S_RECIP, r_sem.at[n], dp, member(dx, c)).start()
 
-    tot_s[...] = recip_own
+    total = jnp.broadcast_to(jnp.sum(tot_s[...], axis=1, keepdims=True), (ROWS, 128))
+    tot_s[...] = own_valid[...] / total
     g_s[...] = jnp.zeros_like(g_s)
     lane_f = lax.broadcasted_iota(jnp.int32, (1, ROWS), 1).astype(jnp.float32)
 

time: 48 us -> 47.6 us (level)
  no operation moved by 1% of the time
where the time goes in v8:
time: 47.6 us; the launch traced here: 47.5 us
  Pallas kernels  46.9 us (99%)
  local copies, waits for them, and re-layouts  0.6 us (1%)
    pallas_call x1, Pallas kernels, per_device(): pl.pallas_call(kernel, out_shape=pltpu.VMEM((8, DE), f32), in_specs=[pl.B...  46.9 us

profile of v8, /device:TPU:6, one launch (start us, length us, event | category | flops | bytes accessed | tf_op | source)
XLA Modules:
  0.0 47.5 jit_solution(6766501289506160993)
XLA Ops:
  0.0 46.9 %shard_map.55 = f32[8,256]{1,0:T(8,128)S(1)} custom-call(bf16[256,2048]{1,0:T(8,128)(2,1)} %feats_hbm.1, bf16[2048,256]{1,0:T(8,128)(2,1)} %w_hbm.1, s32[1,256]{1,0:T(1,128)} %bitcast.2, s32[1,256]{1,0:T(1,128)} %bitcast.3, s32[16,16]{1,0:T(8,128)} %counts_hbm.1), custom_call_target="tpu_custom_call" | custom-call | tf_op jit(solution)/shard_map/pallas_call | solution.py:398
  46.9 0.6 %copy.7 = f32[8,256]{1,0:T(8,128)} copy(f32[8,256]{1,0:T(8,128)S(1)} %shard_map.55) | data formatting | bytes 16384

commit v9 on v8

--- a/solution.py
+++ b/solution.py
@@ -60,7 +60,8 @@
     def member(dx, c):
         return ((x + dx) % 4) * 4 + zs[c]
 
-    S_META, S_MIDMETA, S_E, S_MID, S_RECIP, S_CORE, S_TWO, S_THREE, S_FOUR = range(9)
+    S_META = S_E = S_RECIP = S_CORE = S_TWO = S_THREE = S_FOUR = 0
+    S_MID = S_MIDMETA = 1
 
     def remote(src, dst, kind, sem, d, p):
         return pltpu.make_async_remote_copy(
@@ -151,7 +152,7 @@
             ).start()
 
     def arrive(dx, c, h):
-        landed(size.at[0:32 + h], sem_of(dx, c, h))
+        landed(size.at[0:64 + 2 * h], sem_of(dx, c, h))
 
     for h in (0, 1):
         go(0, 0, h, "right")
@@ -211,7 +212,7 @@
             go(0, c, h, "left")
 
     def rest(c):
-        landed(size.at[0:65], sem_of(3, c, 1))
+        landed(size.at[0:130], sem_of(3, c, 1))
         scores(3, c)
         scores(1, c)
 
@@ -256,7 +257,7 @@
     rest(0)
     scores(2, 0)
     scores(0, 2)
-    landed(size.at[0:130], sem_of(3, 1, 0))
+    landed(size.at[0:260], sem_of(3, 1, 0))
     scores(3, 1)
     scores(1, 1)
     arrive(3, 2, 0)
@@ -267,9 +268,9 @@
     scores(0, 3)
     rest(2)
     for c in (1, 2, 3):
-        landed(size.at[0:65], sem_of(2, c, 0))
+        landed(size.at[0:130], sem_of(2, c, 0))
         scores(2, c)
-    landed(size.at[0:130], sem_of(3, 3, 0))
+    landed(size.at[0:260], sem_of(3, 3, 0))
     scores(3, 3)
     scores(1, 3)
 
@@ -380,15 +381,8 @@
     def sent(ref, kind):
         remote(ref, ref, kind, r4_sem.at[0], dp, pool).wait_send()
 
-    sent(meta.at[0:14], S_META)
-    pl.when(middle)(lambda: sent(meta.at[0:2], S_MIDMETA))
-    sent(e_all.at[0:14], S_E)
-    pl.when(middle)(lambda: sent(e_all.at[0:2], S_MID))
-    sent(recips.at[0:15], S_RECIP)
-    sent(core_send, S_CORE)
-    sent(send2.at[0:3], S_TWO)
-    sent(send3.at[0:3], S_THREE)
-    sent(send4.at[0:7], S_FOUR)
+    sent(size.at[0:14 * 128 + 14 * 2 + 15 + 4 * 128 + 12 * 32 + 3 * 32 + 7 * 8], S_E)
+    pl.when(middle)(lambda: sent(size.at[0:2 * 128 + 2 * 2], S_MID))
 
 
 def per_device(feats, tower_w, partners, popularity_buckets, row_counts):
@@ -419,7 +413,7 @@
             vmem((ROWS, 128), f32),
             vmem((ROWS, 128), f32),
             vmem((ROWS, DE), f32),
-            vmem((130, 2, ROWS), f32),
+            vmem((2883, 1, ROWS), f32),
             vmem((4, 256, DE), bf16),
             vmem((4, 256, DE), bf16),
             vmem((4, 4, 64, DE), f32),
@@ -431,7 +425,7 @@
             vmem((8, 8, DE), f32),
             dma((KC,)),
             dma((3,)),
-            dma((9,)),
+            dma((2,)),
             dma((19,)),
             dma((4,)),
             dma((4,)),

time: 47.6 us -> 47.5 us (level)
  no operation moved by 1% of the time
where the time goes in v9:
time: 47.5 us; the launch traced here: 47.4 us
  Pallas kernels  46.8 us (99%)
  local copies, waits for them, and re-layouts  0.6 us (1%)
    pallas_call x1, Pallas kernels, per_device(): pl.pallas_call(kernel, out_shape=pltpu.VMEM((8, DE), f32), in_specs=[pl.B...  46.8 us

profile of v9, /device:TPU:6, one launch (start us, length us, event | category | flops | bytes accessed | tf_op | source)
XLA Modules:
  0.0 47.4 jit_solution(13273362933952765720)
XLA Ops:
  0.0 46.8 %shard_map.55 = f32[8,256]{1,0:T(8,128)S(1)} custom-call(bf16[256,2048]{1,0:T(8,128)(2,1)} %feats_hbm.1, bf16[2048,256]{1,0:T(8,128)(2,1)} %w_hbm.1, s32[1,256]{1,0:T(1,128)} %bitcast.2, s32[1,256]{1,0:T(1,128)} %bitcast.3, s32[16,16]{1,0:T(8,128)} %counts_hbm.1), custom_call_target="tpu_custom_call" | custom-call | tf_op jit(solution)/shard_map/pallas_call | solution.py:392
  46.8 0.6 %copy.7 = f32[8,256]{1,0:T(8,128)} copy(f32[8,256]{1,0:T(8,128)S(1)} %shard_map.55) | data formatting | bytes 16384

commit v10 on v9

--- a/solution.py
+++ b/solution.py
@@ -92,8 +92,8 @@
         pltpu.make_async_copy(w_hbm.at[cols, :], w_v.at[cols, :], in_sem.at[k]).start()
     small = [
         pltpu.make_async_copy(part_hbm, part_v, small_sem.at[0]),
-        pltpu.make_async_copy(buck_hbm, buck_v, small_sem.at[1]),
-        pltpu.make_async_copy(counts_hbm, counts_v, small_sem.at[2]),
+        pltpu.make_async_copy(buck_hbm, buck_v, small_sem.at[0]),
+        pltpu.make_async_copy(counts_hbm, counts_v, small_sem.at[1]),
     ]
     for c in small:
         c.start()
@@ -111,8 +111,8 @@
     inv_s[...] = jnp.broadcast_to(inv_norm, (ROWS, 128))
     e_all[pool] = normed.astype(jnp.bfloat16)
 
-    for c in small:
-        c.wait()
+    pltpu.make_async_copy(size.at[0:2], size.at[0:2], small_sem.at[0]).wait()
+    small[2].wait()
     cnt = counts_v[dp, pool]
     lane = lax.broadcasted_iota(jnp.int32, (1, ROWS), 1)
     valid = lane < cnt
@@ -424,7 +424,7 @@
             vmem((8, 8, DE), f32),
             vmem((8, 8, DE), f32),
             dma((KC,)),
-            dma((3,)),
+            dma((2,)),
             dma((2,)),
             dma((19,)),
             dma((4,)),

time: 47.5 us -> 47.5 us (level)
  no operation moved by 1% of the time
where the time goes in v10:
time: 47.5 us; the launch traced here: 47.4 us
  Pallas kernels  46.8 us (99%)
  local copies, waits for them, and re-layouts  0.6 us (1%)
    pallas_call x1, Pallas kernels, per_device(): pl.pallas_call(kernel, out_shape=pltpu.VMEM((8, DE), f32), in_specs=[pl.B...  46.8 us

profile of v10, /device:TPU:6, one launch (start us, length us, event | category | flops | bytes accessed | tf_op | source)
XLA Modules:
  0.0 47.4 jit_solution(382434337328974028)
XLA Ops:
  0.0 46.8 %shard_map.55 = f32[8,256]{1,0:T(8,128)S(1)} custom-call(bf16[256,2048]{1,0:T(8,128)(2,1)} %feats_hbm.1, bf16[2048,256]{1,0:T(8,128)(2,1)} %w_hbm.1, s32[1,256]{1,0:T(1,128)} %bitcast.2, s32[1,256]{1,0:T(1,128)} %bitcast.3, s32[16,16]{1,0:T(8,128)} %counts_hbm.1), custom_call_target="tpu_custom_call" | custom-call | tf_op jit(solution)/shard_map/pallas_call | solution.py:392
  46.8 0.6 %copy.7 = f32[8,256]{1,0:T(8,128)} copy(f32[8,256]{1,0:T(8,128)S(1)} %shard_map.55) | data formatting | bytes 16384
